TPU v7x, 512 devices: a whole 4x4x16 slice. The times are simulated.
512 devices in a mesh: event: 8 (over y, core), tile: 64 (over x, z).
Axes of the slice: x: 4, y: 4, z: 16, core: 2. Of those that a mesh axis runs over, the one named last changes fastest.
Arguments:
- surface_start: float32 [8, 512, 8192], P('event', 'tile'), may hold values from -6 to 6
- east_start: float32 [8, 512, 8192], P('event', 'tile'), may hold values from -5 to 5
- north_start: float32 [8, 512, 8192], P('event', 'tile'), may hold values from -5 to 5
- still_depth: float32 [512, 8192], P('tile'), may hold values from 1 to 4
- roughness: float32 [512, 8192], P('tile'), may hold values from 0.5 to 2
- wet_masks: int32 [8, 2, 512, 8192], P('event', None, 'tile'), may hold values 0 or 1
- gauge_tiles: int32 [8, 16384, 1], P('event', 'tile'), may hold values from 0 to 63; in each aligned block of 256 rows (0 to 255, 256 to 511, ..., all dimensions but the last counted through in order) at most 8 rows name the same one
- gauge_cells: int32 [8, 16384], P('event', 'tile'), may hold values from 0 to 65535
- gauge_values: float32 [8, 16384], P('event', 'tile'), may hold values from -6 to 6
- survey_surface: float32 [8, 512, 8192], P('event', 'tile'), may hold values from -6 to 6
Outputs:
- roughness_grad: float32 [512, 8192], P('tile', 'event')
Inputs may be any that keep to these rules, and one draw needn't show every extreme that they name: `gauge_tiles`: of the gauges of one event listed on one strip, at most 8 lie in any one strip, and some strip receives exactly 8.
All inputs are finite; a program needn't handle non-finite values. No bound on the sum of `wet_masks` on one device may be relied on, other than what follows from the above.
Results may differ from a plain program's by a relative error of at most 0.0003.
Values sent between devices are 32-bit elements; how exact they have to be, the bound alone decides.
No kernel may reach another device: no remote copies, remote signals or barrier semaphores. Data moves between devices by JAX's collectives and lax.ppermute only.
A program may use at most 64 MiB of HBM per device.

v0:
```python
import jax
import jax.numpy as jnp
from jax import lax
from jax.sharding import PartitionSpec as P

STEPS = 2


def shifted(value, axis, steps):
    count = lax.axis_size(axis)
    initial, last = (max(0, -steps), min(count, count - steps))
    return lax.ppermute(value, axis, [(source, source + steps) for source in range(initial, last)])


def padded_2(cells, sides, width):
    for axis, dim in sides:
        count = lax.axis_size(axis)
        ends = count - 1
        head = lax.slice_in_dim(cells, 0, width, axis=dim)
        tail = lax.slice_in_dim(cells, cells.shape[dim] - width, cells.shape[dim], axis=dim)
        cells = jnp.concatenate(
            [
                lax.ppermute(tail, axis, [(i, (i + 1) % count) for i in range(ends)]),
                cells,
                lax.ppermute(head, axis, [((i + 1) % count, i) for i in range(ends)]),
            ],
            axis=dim,
        )
    return cells


def interior(field):
    return field[1:-1]


def across(field):
    padded = jnp.pad(field, ((0, 0), (1, 1)))
    return padded[:, 2:] - padded[:, :-2]


def along(field):
    return field[2:] - field[:-2]


def advance(surface, east, north, depth_rows, rough_rows, wetness):
    depth_inner = interior(depth_rows)
    depth_safe = jnp.where(depth_inner > 0, depth_inner, 1.0)
    east_inner = interior(east)
    north_inner = interior(north)
    speed = jnp.sqrt(east_inner * east_inner + north_inner * north_inner + 1.0)
    rough_inner = interior(rough_rows)
    friction = 1.0 + 2.0 * rough_inner * rough_inner * speed / depth_safe ** (4.0 / 3.0)
    wet_inner = interior(wetness)
    new_east = wet_inner * (east_inner - 0.2 * depth_inner * across(interior(surface))) / friction
    new_north = wet_inner * (north_inner - 0.2 * depth_inner * along(surface)) / friction
    new_surface = interior(interior(surface)) - 0.25 * interior(wet_inner) * (
        interior(across(new_east)) + along(new_north)
    )
    return (new_surface, interior(new_east), interior(new_north))


def fold_rims(stacked, width):
    upper = stacked[:, :width]
    lower = stacked[:, stacked.shape[1] - width :]
    inner = stacked[:, width : stacked.shape[1] - width]
    from_below = shifted(upper, "tile", -1)
    from_above = shifted(lower, "tile", 1)
    inner = inner.at[:, inner.shape[1] - width :].add(from_below)
    return inner.at[:, :width].add(from_above)


def per_device(
    surface_start,
    east_start,
    north_start,
    still_depth,
    roughness,
    wet_masks,
    gauge_tiles,
    gauge_cells,
    gauge_values,
    survey_surface,
):
    row_count, col_count = still_depth.shape
    wet_float = wet_masks[0].astype(jnp.float32)
    statics = jnp.stack((still_depth, roughness))
    stored = []
    width = 2
    static_pad = padded_2(statics, (("tile", 1),), 2)
    surface, east, north = (surface_start[0], east_start[0], north_start[0])
    for step_index in range(STEPS):
        padded = padded_2(
            jnp.stack((surface, east, north, wet_float[step_index])), (("tile", 1),), 2
        )
        record = (padded[0], padded[1], padded[2], static_pad[0], static_pad[1], padded[3])
        stored.append(record)
        surface, east, north = advance(*record)
    strip_tiles = gauge_tiles[0, :, 0]
    tile_count = lax.axis_size("tile")
    listed = strip_tiles.shape[0]
    capacity = max(2, 2 * listed // tile_count)
    onehot = (strip_tiles[:, None] == jnp.arange(tile_count, dtype=jnp.int32)[None, :]).astype(
        jnp.int32
    )
    before = jnp.cumsum(onehot, axis=0) - onehot
    rank = jnp.sum(onehot * before, axis=1)
    slot = strip_tiles * capacity + rank
    cell_count = row_count * col_count
    send_cells = (
        jnp.full((tile_count * capacity,), cell_count, jnp.int32).at[slot].set(gauge_cells[0])
    )
    send_values = jnp.zeros((tile_count * capacity,), jnp.float32).at[slot].set(gauge_values[0])
    got_cells, got_values = (
        lax.all_to_all(
            send_cells.reshape(tile_count, capacity),
            "tile",
            split_axis=0,
            concat_axis=0,
            tiled=True,
        ),
        lax.all_to_all(
            send_values.reshape(tile_count, capacity),
            "tile",
            split_axis=0,
            concat_axis=0,
            tiled=True,
        ),
    )
    flat_cells = got_cells.reshape(-1)
    valid = flat_cells < cell_count
    seen = jnp.take(surface.reshape(-1), flat_cells, mode="fill", fill_value=0.0)
    missing = jnp.where(valid, seen - got_values.reshape(-1), 0.0)
    gauge_sense = (
        jnp.zeros((cell_count,), jnp.float32)
        .at[flat_cells]
        .add(missing, mode="drop")
        .reshape(row_count, col_count)
    )
    sense_surface = gauge_sense + (surface - survey_surface[0])
    sense_east = jnp.zeros_like(sense_surface)
    sense_north = jnp.zeros_like(sense_surface)
    rough_sense = jnp.zeros((row_count + 2 * width, col_count), jnp.float32)
    for step_index in reversed(range(STEPS)):
        surface_in, east_in, north_in, depth_rows, rough_rows, wetness = stored[step_index]

        def local_step(surface_arg, east_arg, north_arg, rough_arg):
            return advance(surface_arg, east_arg, north_arg, depth_rows, rough_arg, wetness)

        outputs, pullback = jax.vjp(local_step, surface_in, east_in, north_in, rough_rows)
        back_surface, back_east, back_north, back_rough = pullback(
            (sense_surface, sense_east, sense_north)
        )
        rough_sense = rough_sense + back_rough
        if step_index > 0:
            folded = fold_rims(jnp.stack((back_surface, back_east, back_north)), 2)
            sense_surface, sense_east, sense_north = (folded[0], folded[1], folded[2])
    local_grad = fold_rims(rough_sense[None], width)[0]
    total = lax.psum(local_grad, "event")
    share = col_count // lax.axis_size("event")
    return lax.dynamic_slice_in_dim(total, lax.axis_index("event") * share, share, 1)


def solution(mesh):
    placed = (
        P("event", "tile", None),
        P("event", "tile", None),
        P("event", "tile", None),
        P("tile", None),
        P("tile", None),
        P("event", None, "tile", None),
        P("event", "tile", None),
        P("event", "tile"),
        P("event", "tile"),
        P("event", "tile", None),
    )
    return jax.shard_map(
        per_device, mesh=mesh, in_specs=placed, out_specs=P("tile", "event"), check_vma=False
    )
```

profile of v0, /device:TPU:2, one launch (start us, length us, event | category | flops | bytes accessed | tf_op | source)
XLA Modules:
  0.0 217.5 jit_solution(9492636156233918174)
XLA Ops:
  6.5 1.4 pad_maximum_fusion.31
  7.9 3.8 %collective-permute-start = (f32[2,2,8192]{2,1,0:T(2,128)S(1)}, f32[2,2,8192]{2,1,0:T(2,128)S(1)}, u32[]{:S(2)}, u32[]{:S(2)}) collective-permute-start(f32[2,2,8192]{2,1,0:T(2,128)S(1)} %get-tuple-element.102), channel_id=1, source_target_pairs={{0,1},{1,2},{2,3},{3,4},{4,5},{5,6},{6,7},{7,8},{8,9},{9,10},{10,1... | collective-permute-start | bytes 393224 | tf_op jit(solution)/shard_map/ppermute | solution.py:23
  11.7 9.5 %collective-permute-start.1 = (f32[2,2,8192]{2,1,0:T(2,128)S(1)}, f32[2,2,8192]{2,1,0:T(2,128)}, u32[]{:S(2)}, u32[]{:S(2)}) collective-permute-start(f32[2,2,8192]{2,1,0:T(2,128)S(1)} %get-tuple-element.103), channel_id=1, source_target_pairs={{1,0},{2,1},{3,2},{4,3},{5,4},{6,5},{7,6},{8,7},{9,8},{10,9},{11,1... | collective-permute-start | bytes 393224 | tf_op jit(solution)/shard_map/ppermute | solution.py:25
  24.2 1.6 scatter_custom_fusion
  26.5 12.4 %all-to-all-start = ((s32[64,1,8]{2,1,0:T(1,128)}), s32[64,1,8]{2,1,0:T(1,128)S(1)}, u32[]{:S(2)}, u32[]{:S(2)}) async-start(s32[64,1,8]{2,1,0:T(1,128)} %bitcast.12), calls=%async_computation | async-start | bytes 65536 | tf_op jit(solution)/shard_map/all_to_all | solution.py:114
  40.0 1.6 scatter_custom_fusion.1
  42.3 10.1 %all-to-all-done = s32[64,1,8]{2,1,0:T(1,128)S(1)} async-done(((s32[64,1,8]{2,1,0:T(1,128)}), s32[64,1,8]{2,1,0:T(1,128)S(1)}, u32[]{:S(2)}, u32[]{:S(2)}) %all-to-all-start) | async-done | bytes 2080 | tf_op jit(solution)/shard_map/all_to_all | solution.py:114
  52.4 5.5 %all-to-all-start.1 = ((f32[64,1,8]{2,1,0:T(1,128)}), f32[64,1,8]{2,1,0:T(1,128)S(1)}, u32[]{:S(2)}, u32[]{:S(2)}) async-start(f32[64,1,8]{2,1,0:T(1,128)} %bitcast.32), calls=%async_computation.1 | async-start | bytes 65536 | tf_op jit(solution)/shard_map/all_to_all | solution.py:121
  58.9 3.4 %collective-permute-start.2 = (f32[4,2,8192]{2,1,0:T(2,128)}, f32[4,2,8192]{2,1,0:T(2,128)S(1)}, u32[]{:S(2)}, u32[]{:S(2)}) collective-permute-start(f32[4,2,8192]{2,1,0:T(2,128)} %get-tuple-element.88), channel_id=1, source_target_pairs={{0,1},{1,2},{2,3},{3,4},{4,5},{5,6},{6,7},{7,8},{8,9},{9,10},{10,1... | collective-permute-start | bytes 786440 | tf_op jit(solution)/shard_map/ppermute | solution.py:23
  62.2 4.6 %collective-permute-start.3 = (f32[4,2,8192]{2,1,0:T(2,128)}, f32[4,2,8192]{2,1,0:T(2,128)S(1)}, u32[]{:S(2)}, u32[]{:S(2)}) collective-permute-start(f32[4,2,8192]{2,1,0:T(2,128)} %get-tuple-element.89), channel_id=1, source_target_pairs={{1,0},{2,1},{3,2},{4,3},{5,4},{6,5},{7,6},{8,7},{9,8},{10,9},{11,1... | collective-permute-start | bytes 786440 | tf_op jit(solution)/shard_map/ppermute | solution.py:25
  68.3 3.0 %all-to-all-done.1 = f32[64,1,8]{2,1,0:T(1,128)S(1)} async-done(((f32[64,1,8]{2,1,0:T(1,128)}), f32[64,1,8]{2,1,0:T(1,128)S(1)}, u32[]{:S(2)}, u32[]{:S(2)}) %all-to-all-start.1) | async-done | bytes 2080 | tf_op jit(solution)/shard_map/all_to_all | solution.py:121
  72.7 1.3 pad_maximum_fusion.3
  75.8 2.0 fusion.58
  77.9 1.4 pad_slice_fusion.3
  79.6 2.6 %collective-permute-start.4 = (f32[4,2,8192]{2,1,0:T(2,128)S(1)}, f32[4,2,8192]{2,1,0:T(2,128)S(1)}, u32[]{:S(2)}, u32[]{:S(2)}) collective-permute-start(f32[4,2,8192]{2,1,0:T(2,128)S(1)} %get-tuple-element.86), channel_id=1, source_target_pairs={{0,1},{1,2},{2,3},{3,4},{4,5},{5,6},{6,7},{7,8},{8,9},{9,10},{10,1... | collective-permute-start | bytes 786440 | tf_op jit(solution)/shard_map/ppermute | solution.py:23
  82.2 5.5 %collective-permute-start.5 = (f32[4,2,8192]{2,1,0:T(2,128)S(1)}, f32[4,2,8192]{2,1,0:T(2,128)S(1)}, u32[]{:S(2)}, u32[]{:S(2)}) collective-permute-start(f32[4,2,8192]{2,1,0:T(2,128)S(1)} %get-tuple-element.87), channel_id=1, source_target_pairs={{1,0},{2,1},{3,2},{4,3},{5,4},{6,5},{7,6},{8,7},{9,8},{10,9},{11,1... | collective-permute-start | bytes 786440 | tf_op jit(solution)/shard_map/ppermute | solution.py:25
  87.8 2.2 %collective-permute-done.4 = f32[4,2,8192]{2,1,0:T(2,128)S(1)} collective-permute-done((f32[4,2,8192]{2,1,0:T(2,128)S(1)}, f32[4,2,8192]{2,1,0:T(2,128)S(1)}, u32[]{:S(2)}, u32[]{:S(2)}) %collective-permute-start.4) | collective-permute-done | bytes 262176 | tf_op jit(solution)/shard_map/ppermute | solution.py:23
  90.0 1.5 collective-permute-done.5
  91.8 2.0 fusion.55
  97.1 3.1 %gather_fusion = f32[512]{0:T(512)S(1)} fusion(f32[65536]{0:T(1024)S(1)} %bitcast.247, s32[1024]{0:T(1024)S(1)} %pad_clamp_fusion), kind=kCustom, calls=%fused_computation | custom fusion | bytes 6144 | tf_op jit(solution)/shard_map/jit(_take)/gather | solution.py:131
  100.3 3.9 %scatter_custom_fusion.2 = f32[65536]{0:T(1024)} fusion(s32[512]{0:T(512)S(1)} %bitcast.260, f32[512]{0:T(512)S(1)} %subtract_select_fusion, f32[]{:T(128)} %constant.144.clone.1), kind=kCustom, calls=%fused_computation.127 | custom fusion | flops 512 | bytes 262148 | tf_op jit(solution)/shard_map/scatter-add | solution.py:136
  105.3 1.3 fusion.53
  106.8 1.7 fusion
  110.2 6.5 %collective-permute-start.6 = (f32[3,2,8192]{2,1,0:T(2,128)S(1)}, f32[3,2,8192]{2,1,0:T(2,128)S(1)}, u32[]{:S(2)}, u32[]{:S(2)}) collective-permute-start(f32[3,2,8192]{2,1,0:T(2,128)S(1)} %get-tuple-element.85), channel_id=1, source_target_pairs={{1,0},{2,1},{3,2},{4,3},{5,4},{6,5},{7,6},{8,7},{9,8},{10,9},{11,1... | collective-permute-start | bytes 589832 | tf_op jit(solution)/shard_map/ppermute | solution.py:12
  116.9 2.1 collective-permute-start.7
  120.1 6.6 %collective-permute-done.7 = f32[3,2,8192]{2,1,0:T(2,128)S(1)} collective-permute-done((f32[3,2,8192]{2,1,0:T(2,128)S(1)}, f32[3,2,8192]{2,1,0:T(2,128)S(1)}, u32[]{:S(2)}, u32[]{:S(2)}) %collective-permute-start.7) | collective-permute-done | bytes 196640 | tf_op jit(solution)/shard_map/ppermute | solution.py:12
  127.1 1.5 fusion.1
  128.9 1.9 collective-permute-start.8
  130.8 3.9 %collective-permute-start.9 = (f32[1,2,8192]{2,1,0:T(2,128)S(1)}, f32[1,2,8192]{2,1,0:T(2,128)S(1)}, u32[]{:S(2)}, u32[]{:S(2)}) collective-permute-start(f32[1,2,8192]{2,1,0:T(2,128)S(1)} %get-tuple-element.92), channel_id=1, source_target_pairs={{0,1},{1,2},{2,3},{3,4},{4,5},{5,6},{6,7},{7,8},{8,9},{9,10},{10,1... | collective-permute-start | bytes 196616 | tf_op jit(solution)/shard_map/ppermute | solution.py:12
  135.1 4.0 %collective-permute-done.9 = f32[1,2,8192]{2,1,0:T(2,128)S(1)} collective-permute-done((f32[1,2,8192]{2,1,0:T(2,128)S(1)}, f32[1,2,8192]{2,1,0:T(2,128)S(1)}, u32[]{:S(2)}, u32[]{:S(2)}) %collective-permute-start.9) | collective-permute-done | bytes 65568 | tf_op jit(solution)/shard_map/ppermute | solution.py:12
  139.9 69.4 %all-reduce.30.cloned.1.call-done = f32[8,8192]{1,0:T(8,128)} async-done(((f32[8,8192]{1,0:T(8,128)}), f32[8,8192]{1,0:T(8,128)}) %all-reduce.30.cloned.1.call-update) | async-done | bytes 262160 | tf_op jit(solution)/shard_map/psum | solution.py:158
  209.3 1.4 constant_dynamic-slice_fusion
  (111 shorter events, 20.9 us)
Async XLA Ops:
  6.5 51.3 %copy-start.9 = (f32[1,8,8192]{2,1,0:T(8,128)S(1)}, f32[1,8,8192]{2,1,0:T(8,128)}, u32[]{:S(2)}) copy-start(f32[1,8,8192]{2,1,0:T(8,128)} %param.18) | copy-start | bytes 786436
  6.5 51.3 %copy-start.12 = (f32[1,8,8192]{2,1,0:T(8,128)S(1)}, f32[1,8,8192]{2,1,0:T(8,128)}, u32[]{:S(2)}) copy-start(f32[1,8,8192]{2,1,0:T(8,128)} %param.19) | copy-start | bytes 786436
  6.5 51.4 %copy-start.10 = (f32[1,8,8192]{2,1,0:T(8,128)S(1)}, f32[1,8,8192]{2,1,0:T(8,128)}, u32[]{:S(2)}) copy-start(f32[1,8,8192]{2,1,0:T(8,128)} %param.20) | copy-start | bytes 786436
  7.9 64.8 %collective-permute-start = (f32[2,2,8192]{2,1,0:T(2,128)S(1)}, f32[2,2,8192]{2,1,0:T(2,128)S(1)}, u32[]{:S(2)}, u32[]{:S(2)}) collective-permute-start(f32[2,2,8192]{2,1,0:T(2,128)S(1)} %get-tuple-element.102), channel_id=1, source_target_pairs={{0,1},{1,2},{2,3},{3,4},{4,5},{5,6},{6,7},{7,8},{8,9},{9,10},{10,1... | collective-permute-start | bytes 393224 | tf_op jit(solution)/shard_map/ppermute | solution.py:23
  11.7 61.0 %collective-permute-start.1 = (f32[2,2,8192]{2,1,0:T(2,128)S(1)}, f32[2,2,8192]{2,1,0:T(2,128)}, u32[]{:S(2)}, u32[]{:S(2)}) collective-permute-start(f32[2,2,8192]{2,1,0:T(2,128)S(1)} %get-tuple-element.103), channel_id=1, source_target_pairs={{1,0},{2,1},{3,2},{4,3},{5,4},{6,5},{7,6},{8,7},{9,8},{10,9},{11,1... | collective-permute-start | bytes 393224 | tf_op jit(solution)/shard_map/ppermute | solution.py:25
  26.5 25.9 %all-to-all-start = ((s32[64,1,8]{2,1,0:T(1,128)}), s32[64,1,8]{2,1,0:T(1,128)S(1)}, u32[]{:S(2)}, u32[]{:S(2)}) async-start(s32[64,1,8]{2,1,0:T(1,128)} %bitcast.12), calls=%async_computation | async-start | bytes 65536 | tf_op jit(solution)/shard_map/all_to_all | solution.py:114
  40.0 39.3 %copy-start.2 = (f32[1,2,8,8192]{3,2,1,0:T(8,128)}, f32[1,2,8,8192]{3,2,1,0:T(8,128)S(1)}, u32[]{:S(2)}) copy-start(f32[1,2,8,8192]{3,2,1,0:T(8,128)S(1)} %convert_element_type.19) | copy-start | bytes 1572868
  52.4 19.0 %all-to-all-start.1 = ((f32[64,1,8]{2,1,0:T(1,128)}), f32[64,1,8]{2,1,0:T(1,128)S(1)}, u32[]{:S(2)}, u32[]{:S(2)}) async-start(f32[64,1,8]{2,1,0:T(1,128)} %bitcast.32), calls=%async_computation.1 | async-start | bytes 65536 | tf_op jit(solution)/shard_map/all_to_all | solution.py:121
  57.8 151.5 %all-reduce.30.cloned.1.call-start = ((), (), s32[]{:S(2)}) async-start(), calls=%async_computation.2 | async-start | bytes 524288 | tf_op jit(solution)/shard_map/psum | solution.py:158
  58.9 15.1 %collective-permute-start.2 = (f32[4,2,8192]{2,1,0:T(2,128)}, f32[4,2,8192]{2,1,0:T(2,128)S(1)}, u32[]{:S(2)}, u32[]{:S(2)}) collective-permute-start(f32[4,2,8192]{2,1,0:T(2,128)} %get-tuple-element.88), channel_id=1, source_target_pairs={{0,1},{1,2},{2,3},{3,4},{4,5},{5,6},{6,7},{7,8},{8,9},{9,10},{10,1... | collective-permute-start | bytes 786440 | tf_op jit(solution)/shard_map/ppermute | solution.py:23
  62.2 11.8 %collective-permute-start.3 = (f32[4,2,8192]{2,1,0:T(2,128)}, f32[4,2,8192]{2,1,0:T(2,128)S(1)}, u32[]{:S(2)}, u32[]{:S(2)}) collective-permute-start(f32[4,2,8192]{2,1,0:T(2,128)} %get-tuple-element.89), channel_id=1, source_target_pairs={{1,0},{2,1},{3,2},{4,3},{5,4},{6,5},{7,6},{8,7},{9,8},{10,9},{11,1... | collective-permute-start | bytes 786440 | tf_op jit(solution)/shard_map/ppermute | solution.py:25
  75.7 2.1 copy-start
  75.8 2.1 copy-start.11
  75.8 2.1 copy-start.13
  75.8 2.1 copy-start.19
  75.8 2.1 copy-start.21
  77.8 1.5 copy-start.7
  79.6 10.4 %collective-permute-start.4 = (f32[4,2,8192]{2,1,0:T(2,128)S(1)}, f32[4,2,8192]{2,1,0:T(2,128)S(1)}, u32[]{:S(2)}, u32[]{:S(2)}) collective-permute-start(f32[4,2,8192]{2,1,0:T(2,128)S(1)} %get-tuple-element.86), channel_id=1, source_target_pairs={{0,1},{1,2},{2,3},{3,4},{4,5},{5,6},{6,7},{7,8},{8,9},{9,10},{10,1... | collective-permute-start | bytes 786440 | tf_op jit(solution)/shard_map/ppermute | solution.py:23
  82.2 9.2 %collective-permute-start.5 = (f32[4,2,8192]{2,1,0:T(2,128)S(1)}, f32[4,2,8192]{2,1,0:T(2,128)S(1)}, u32[]{:S(2)}, u32[]{:S(2)}) collective-permute-start(f32[4,2,8192]{2,1,0:T(2,128)S(1)} %get-tuple-element.87), channel_id=1, source_target_pairs={{1,0},{2,1},{3,2},{4,3},{5,4},{6,5},{7,6},{8,7},{9,8},{10,9},{11,1... | collective-permute-start | bytes 786440 | tf_op jit(solution)/shard_map/ppermute | solution.py:25
  93.9 1.4 copy-start.5
  105.2 1.4 copy-start.6
  105.2 1.4 copy-start.16
  105.3 1.6 copy-start.17
  110.2 9.7 %collective-permute-start.6 = (f32[3,2,8192]{2,1,0:T(2,128)S(1)}, f32[3,2,8192]{2,1,0:T(2,128)S(1)}, u32[]{:S(2)}, u32[]{:S(2)}) collective-permute-start(f32[3,2,8192]{2,1,0:T(2,128)S(1)} %get-tuple-element.85), channel_id=1, source_target_pairs={{1,0},{2,1},{3,2},{4,3},{5,4},{6,5},{7,6},{8,7},{9,8},{10,9},{11,1... | collective-permute-start | bytes 589832 | tf_op jit(solution)/shard_map/ppermute | solution.py:12
  116.8 10.1 %copy-start.4 = (f32[1,2,8,8192]{3,2,1,0:T(8,128)S(1)}, f32[1,2,8,8192]{3,2,1,0:T(8,128)}, u32[]{:S(2)}) copy-start(f32[1,2,8,8192]{3,2,1,0:T(8,128)} %copy-done.2) | copy-start | bytes 1572868
  116.9 9.8 %collective-permute-start.7 = (f32[3,2,8192]{2,1,0:T(2,128)S(1)}, f32[3,2,8192]{2,1,0:T(2,128)S(1)}, u32[]{:S(2)}, u32[]{:S(2)}) collective-permute-start(f32[3,2,8192]{2,1,0:T(2,128)S(1)} %get-tuple-element.84), channel_id=1, source_target_pairs={{0,1},{1,2},{2,3},{3,4},{4,5},{5,6},{6,7},{7,8},{8,9},{9,10},{10,1... | collective-permute-start | bytes 589832 | tf_op jit(solution)/shard_map/ppermute | solution.py:12
  120.1 7.0 %copy-start.1 = (f32[4,12,8192]{2,1,0:T(8,128)S(1)}, f32[4,12,8192]{2,1,0:T(8,128)}, u32[]{:S(2)}) copy-start(f32[4,12,8192]{2,1,0:T(8,128)} %copy-done) | copy-start | bytes 4718596
  120.1 7.0 %copy-start.8 = (f32[10,8192]{1,0:T(8,128)S(1)}, f32[10,8192]{1,0:T(8,128)}, u32[]{:S(2)}) copy-start(f32[10,8192]{1,0:T(8,128)} %copy-done.7) | copy-start | bytes 983044
  120.1 7.0 %copy-start.14 = (f32[10,8192]{1,0:T(8,128)S(1)}, f32[10,8192]{1,0:T(8,128)}, u32[]{:S(2)}) copy-start(f32[10,8192]{1,0:T(8,128)} %get-tuple-element.75) | copy-start | bytes 983044
  120.1 7.0 %copy-start.15 = (f32[10,8192]{1,0:T(8,128)S(1)}, f32[10,8192]{1,0:T(8,128)}, u32[]{:S(2)}) copy-start(f32[10,8192]{1,0:T(8,128)} %get-tuple-element.109) | copy-start | bytes 983044
  128.9 6.2 %collective-permute-start.8 = (f32[1,2,8192]{2,1,0:T(2,128)S(1)}, f32[1,2,8192]{2,1,0:T(2,128)S(1)}, u32[]{:S(2)}, u32[]{:S(2)}) collective-permute-start(f32[1,2,8192]{2,1,0:T(2,128)S(1)} %get-tuple-element.93), channel_id=1, source_target_pairs={{1,0},{2,1},{3,2},{4,3},{5,4},{6,5},{7,6},{8,7},{9,8},{10,9},{11,1... | collective-permute-start | bytes 196616 | tf_op jit(solution)/shard_map/ppermute | solution.py:12
  130.8 8.3 %collective-permute-start.9 = (f32[1,2,8192]{2,1,0:T(2,128)S(1)}, f32[1,2,8192]{2,1,0:T(2,128)S(1)}, u32[]{:S(2)}, u32[]{:S(2)}) collective-permute-start(f32[1,2,8192]{2,1,0:T(2,128)S(1)} %get-tuple-element.92), channel_id=1, source_target_pairs={{0,1},{1,2},{2,3},{3,4},{4,5},{5,6},{6,7},{7,8},{8,9},{9,10},{10,1... | collective-permute-start | bytes 196616 | tf_op jit(solution)/shard_map/ppermute | solution.py:12
  (4 other events, 3.2 us)
Sparse Core Ops, SparseCore 0:
  140.0 69.2 all-reduce.29
where the time goes:
time: 218 us
  waiting for transfers between devices  98 us (45%)
  starting transfers between devices  61.7 us (28%)
  other arithmetic  28.1 us (13%)
  local copies, waits for them, and re-layouts  15.7 us (7%)
  between operations  14.1 us (6%)
    psum x1, waiting for transfers between devices, per_device(): total = lax.psum(local_grad, 'event')  69.4 us
    ppermute x3, starting transfers between devices, padded_2(): lax.ppermute(head, axis, [((i + 1) % count, i) for i in range(ends)])  19.6 us
    ppermute x4, starting transfers between devices, shifted(): lax.ppermute(value, axis, [(source, source + steps) for source in range(i...  14.4 us
    all_to_all x1, starting transfers between devices, per_device(): lax.all_to_all(send_cells.reshape(tile_count, capacity), 'tile', split_ax...  12.4 us
    ppermute x4, waiting for transfers between devices, shifted(): lax.ppermute(value, axis, [(source, source + steps) for source in range(i...  11.8 us
    all_to_all x1, waiting for transfers between devices, per_device(): lax.all_to_all(send_cells.reshape(tile_count, capacity), 'tile', split_ax...  10.1 us
    ppermute x3, starting transfers between devices, padded_2(): lax.ppermute(tail, axis, [(i, (i + 1) % count) for i in range(ends)])  9.78 us
    all_to_all x1, starting transfers between devices, per_device(): lax.all_to_all(send_values.reshape(tile_count, capacity), 'tile', split_a...  5.45 us
  transfers between devices with their start and end apart: 13, of which 9 were waited for; matrix products, arithmetic and copies ran while one was open for 6% of the time, Pallas kernels for 0%

commit v1 on v0

v1 whole, which is shorter than its diff:
```python
import functools
import jax
import jax.numpy as jnp
from jax import lax
from jax.experimental import pallas as pl
from jax.experimental.pallas import tpu as pltpu
from jax.sharding import PartitionSpec as P

LANES = 128
ROWS = 8
STEP = 4
RIM1 = ("s0", "v1", "b", "s1", "r", "u1", "k", "sv")
RIM2 = ("s1", "w0", "v2", "h", "u2", "sv")
RIM3 = ("v2", "h", "s2", "sv")
SENT = tuple((1, x) for x in RIM1) + tuple((2, x) for x in RIM2) + tuple((3, x) for x in RIM3)
SLOT = {key: i for i, key in enumerate(SENT)}
PASS = ("s2_1", "s2_2", "s2_3", "y1", "w0")


def masks(rows):
    lane = lax.broadcasted_iota(jnp.int32, (rows, LANES), 1)
    sub = lax.broadcasted_iota(jnp.int32, (rows, LANES), 0) & (ROWS - 1)
    return lane, sub


def across(ref, c, n, lane, lead=ROWS):
    x = ref[lead + ROWS * c : lead + ROWS * (c + n), :]
    left = ref[ROWS * c : ROWS * (c + n), :]
    right = ref[2 * lead + ROWS * c : 2 * lead + ROWS * (c + n), :]
    ahead = pltpu.roll(jnp.where(lane == 0, right, x), LANES - 1, 1)
    behind = pltpu.roll(jnp.where(lane == LANES - 1, left, x), 1, 1)
    return ahead - behind


def along(ref, rim, c, n, sub):
    down = ref[ROWS + 1 + ROWS * c : ROWS + 1 + ROWS * (c + n), :]
    up = ref[ROWS - 1 + ROWS * c : ROWS - 1 + ROWS * (c + n), :]
    edge = 0.0 if rim is None else rim[ROWS * c : ROWS * (c + n), :]
    return jnp.where(sub == ROWS - 1, edge, down) - jnp.where(sub == 0, edge, up)


def across_dense(x, scr, lane):
    tiles = x.shape[0]
    scr[ROWS : ROWS + tiles, :] = x
    right = scr[ROWS + 1 : ROWS + 1 + tiles, :]
    left = scr[ROWS - 1 : ROWS - 1 + tiles, :]
    ahead = pltpu.roll(jnp.where(lane == 0, right, x), LANES - 1, 1)
    behind = pltpu.roll(jnp.where(lane == LANES - 1, left, x), 1, 1)
    return ahead - behind


def clear_ends(*refs):
    zero = jnp.zeros((ROWS, LANES), jnp.float32)
    for ref in refs:
        ref[0:ROWS, :] = zero
        ref[ref.shape[0] - ROWS :, :] = zero


def row_of(ref, row, tiles, lead=0):
    return ref[pl.ds(lead + row, tiles, stride=ROWS), :]


def prepare_kernel(
    s0_ref, u0_ref, v0_ref, h_ref, rough_ref, wet_ref, sv_ref,
    down_ref, up_ref, u1_ref, v1_ref, b_ref, q1_ref, k_ref, t0_ref, kr_ref,
    s0p, u1p, v1p, s1p, u2p, v2p, hh, rr, w0q, s2p,
):
    total = s0_ref.shape[0]
    tiles = total // ROWS
    lane, sub = masks(ROWS * STEP)
    clear_ends(s0p, u1p, v1p, s1p, u2p, v2p)
    s0p[ROWS : ROWS + total, :] = s0_ref[...]
    blocks = range(0, tiles, STEP)

    def cut(c, lead=0):
        return slice(lead + ROWS * c, lead + ROWS * (c + STEP))

    for c in blocks:
        at = cut(c)
        depth, rough, east, north = h_ref[at, :], rough_ref[at, :], u0_ref[at, :], v0_ref[at, :]
        wet = wet_ref[at, :].astype(jnp.float32)
        kr = 4.0 * rough * jnp.exp((-4.0 / 3.0) * jnp.log(depth))
        k = 0.5 * kr * rough
        speed = jnp.sqrt(east * east + north * north + 1.0)
        inverse = 1.0 / (1.0 + k * speed)
        y = wet * inverse
        b = 0.2 * depth * y
        u1 = y * east - b * across(s0p, c, STEP, lane)
        v1 = y * north - b * along(s0p, None, c, STEP, sub)
        u1p[cut(c, ROWS), :] = u1
        v1p[cut(c, ROWS), :] = v1
        u1_ref[at, :] = u1
        v1_ref[at, :] = v1
        b_ref[at, :] = b
        k_ref[at, :] = k
        kr_ref[at, :] = kr
        t0_ref[at, :] = kr * speed * inverse
        w0q[at, :] = 0.25 * wet
    for c in blocks:
        at = cut(c)
        quarter = w0q[at, :]
        q1 = s0_ref[at, :] - quarter * across(u1p, c, STEP, lane)
        q1_ref[at, :] = q1
        s1p[cut(c, ROWS), :] = q1 - quarter * along(v1p, None, c, STEP, sub)
    for c in blocks:
        at = cut(c)
        wet = wet_ref[cut(c, total), :].astype(jnp.float32)
        east, north = u1_ref[at, :], v1_ref[at, :]
        depth = 0.2 * h_ref[at, :]
        y = wet / (1.0 + k_ref[at, :] * jnp.sqrt(east * east + north * north + 1.0))
        h = depth * y
        hh[at, :] = h
        rr[at, :] = depth * wet
        u2p[cut(c, ROWS), :] = y * east - h * across(s1p, c, STEP, lane)
        v2p[cut(c, ROWS), :] = y * north - h * along(s1p, None, c, STEP, sub)
    for c in blocks:
        at = cut(c)
        wet = wet_ref[cut(c, total), :].astype(jnp.float32)
        change = across(u2p, c, STEP, lane) + along(v2p, None, c, STEP, sub)
        s2p[at, :] = s1p[cut(c, ROWS), :] - 0.25 * wet * change
    held = {
        (1, "s0"): (s0_ref, 0), (1, "v1"): (v1_ref, 0), (1, "b"): (b_ref, 0), (1, "s1"): (s1p, ROWS),
        (1, "r"): (rr, 0), (1, "u1"): (u1_ref, 0), (1, "k"): (k_ref, 0), (1, "sv"): (sv_ref, 0),
        (2, "s1"): (s1p, ROWS), (2, "w0"): (w0q, 0), (2, "v2"): (v2p, ROWS), (2, "h"): (hh, 0),
        (2, "u2"): (u2p, ROWS), (2, "sv"): (sv_ref, 0),
        (3, "v2"): (v2p, ROWS), (3, "h"): (hh, 0), (3, "s2"): (s2p, 0), (3, "sv"): (sv_ref, 0),
    }
    for key, place in SLOT.items():
        ref, lead = held[key]
        down_ref[place * tiles : (place + 1) * tiles, :] = row_of(ref, ROWS - key[0], tiles, lead)
        up_ref[place * tiles : (place + 1) * tiles, :] = row_of(ref, key[0] - 1, tiles, lead)


def forward_kernel(
    top_ref, bot_ref, s0_ref, h_ref, wet_ref, u1_ref, v1i_ref, b_ref, q1_ref, k_ref, kr_ref,
    v1_ref, s2_ref, u2_ref, v2_ref, y_ref, yh_ref, t2_ref, kk_ref, pass_ref,
    v1p, s1p, u2p, v2p, v1r, s1r, v2r, da, db, dc, dd, de, df,
):
    total = s0_ref.shape[0]
    tiles = total // ROWS
    lane, sub = masks(ROWS * STEP)
    dlane = lax.broadcasted_iota(jnp.int32, (tiles, LANES), 1)
    clear_ends(v1p, s1p, u2p, v2p, da, db, dc, dd, de, df)
    blocks = range(0, tiles, STEP)

    def cut(c, lead=0):
        return slice(lead + ROWS * c, lead + ROWS * (c + STEP))

    sides = ((top_ref, -1.0, 0, (da, db, dc)), (bot_ref, 1.0, ROWS - 1, (dd, de, df)))

    def got(ref, n, name):
        place = SLOT[(n, name)]
        return ref[place * tiles : (place + 1) * tiles, :]

    v1p[ROWS : ROWS + total, :] = v1i_ref[...]
    kept = []
    for ref, sigma, edge, scr in sides:
        b = got(ref, 1, "b")
        delta = b * row_of(s0_ref, edge, tiles)
        v1_1 = got(ref, 1, "v1") + sigma * delta
        v1_e = row_of(v1i_ref, edge, tiles) - sigma * row_of(b_ref, edge, tiles) * got(ref, 1, "s0")
        v1p[pl.ds(ROWS + edge, tiles, stride=ROWS), :] = v1_e
        v1r[pl.ds(edge, tiles, stride=ROWS), :] = v1_1
        bump = got(ref, 2, "w0") * delta
        s1_2 = got(ref, 2, "s1") + bump
        w0_1 = jnp.where(b > 0.0, 1.0, 0.0)
        s1_1 = got(ref, 1, "s1") + (0.25 * sigma) * w0_1 * v1_e
        s1r[pl.ds(edge, tiles, stride=ROWS), :] = s1_1
        r, u1_1, h2, h3 = got(ref, 1, "r"), got(ref, 1, "u1"), got(ref, 2, "h"), got(ref, 3, "h")
        w1_1 = jnp.where(r > 0.0, 1.0, 0.0)
        inverse = 1.0 / (1.0 + got(ref, 1, "k") * jnp.sqrt(u1_1 * u1_1 + v1_1 * v1_1 + 1.0))
        v2i_2 = got(ref, 2, "v2")
        v2_2 = v2i_2 + 0.25 * w0_1 * h2 * v1_e
        v2_3 = got(ref, 3, "v2") + sigma * h3 * bump
        u2_2 = got(ref, 2, "u2") - h2 * across_dense(bump, scr[0], dlane)
        s2_3 = got(ref, 3, "s2") + (0.25 * sigma) * jnp.where(h3 > 0.0, 1.0, 0.0) * (v2_2 - v2i_2)
        u2_1 = (w1_1 * u1_1 - r * across_dense(s1_1, scr[1], dlane)) * inverse
        kept.append((v1_1, s1_1, s1_2, w0_1, w1_1, r, inverse, h2, v2_2, v2_3, u2_1, u2_2, s2_3))
    for c in blocks:
        at = cut(c)
        quarter = 0.25 * wet_ref[at, :].astype(jnp.float32)
        v1_ref[at, :] = v1p[cut(c, ROWS), :]
        s1p[cut(c, ROWS), :] = q1_ref[at, :] - quarter * along(v1p, v1r, c, STEP, sub)
    late = []
    for (ref, sigma, edge, scr), values in zip(sides, kept):
        v1_1, s1_1, s1_2, w0_1, w1_1, r, inverse, h2, v2_2, v2_3, u2_1, u2_2, s2_3 = values
        s1_e = row_of(s1p, edge, tiles, ROWS)
        v2_1 = (w1_1 * v1_1 - sigma * r * (s1_2 - s1_e)) * inverse
        v2r[pl.ds(edge, tiles, stride=ROWS), :] = v2_1
        w1_2 = jnp.where(h2 > 0.0, 0.25, 0.0)
        s2_2 = s1_2 - w1_2 * (across_dense(u2_2, scr[2], dlane) + sigma * (v2_3 - v2_1))
        late.append((s2_2, across_dense(u2_1, scr[0], dlane)))
    for c in blocks:
        at = cut(c)
        wet = wet_ref[cut(c, total), :].astype(jnp.float32)
        east, north = u1_ref[at, :], v1_ref[at, :]
        speed2 = east * east + north * north + 1.0
        slow = lax.rsqrt(speed2)
        speed = speed2 * slow
        k = k_ref[at, :]
        inverse = 1.0 / (1.0 + k * speed)
        y = wet * inverse
        yh = 0.2 * h_ref[at, :] * y
        u2 = y * east - yh * across(s1p, c, STEP, lane)
        v2 = y * north - yh * along(s1p, s1r, c, STEP, sub)
        u2p[cut(c, ROWS), :] = u2
        v2p[cut(c, ROWS), :] = v2
        u2_ref[at, :] = u2
        v2_ref[at, :] = v2
        y_ref[at, :] = y
        yh_ref[at, :] = yh
        t2_ref[at, :] = kr_ref[at, :] * speed * inverse
        kk_ref[at, :] = k * inverse * slow
    for c in blocks:
        at = cut(c)
        wet = wet_ref[cut(c, total), :].astype(jnp.float32)
        change = across(u2p, c, STEP, lane) + along(v2p, v2r, c, STEP, sub)
        s2_ref[at, :] = s1p[cut(c, ROWS), :] - 0.25 * wet * change
    for d, ((ref, sigma, edge, scr), values, more) in enumerate(zip(sides, kept, late)):
        v1_1, s1_1, s1_2, w0_1, w1_1, r, inverse, h2, v2_2, v2_3, u2_1, u2_2, s2_3 = values
        s2_2, du2_1 = more
        v2_e = row_of(v2p, edge, tiles, ROWS)
        s2_1 = s1_1 - 0.25 * w1_1 * (du2_1 + sigma * (v2_2 - v2_e))
        for i, value in enumerate((s2_1, s2_2, s2_3, r * inverse, w0_1)):
            first = (d * len(PASS) + i) * tiles
            pass_ref[first : first + tiles, :] = value


def gauge_fields(places, lanes, values, rows):
    grid = lax.broadcasted_iota(jnp.int32, (rows, LANES), 0)
    lane = lax.broadcasted_iota(jnp.int32, (LANES, LANES), 0)
    left, right = [], []
    for place, at, value in zip(places, lanes, values):
        left.append(jnp.where(grid == place, 1.0, 0.0).astype(jnp.bfloat16))
        hit = lane == at
        high = value.astype(jnp.bfloat16).astype(jnp.float32)
        rest = value - high
        middle = rest.astype(jnp.bfloat16).astype(jnp.float32)
        low = rest - middle
        parts = [jnp.where(hit, part, 0.0).astype(jnp.bfloat16) for part in (high, middle, low)]
        parts.append(jnp.where(hit, 1.0, 0.0).astype(jnp.bfloat16))
        right.append(jnp.concatenate(parts, axis=0))
    out = lax.dot_general(
        jnp.concatenate(left, axis=1), jnp.concatenate(right, axis=1), (((1,), (1,)), ((), ())),
        preferred_element_type=jnp.float32,
    )
    summed = out[:, :LANES] + out[:, LANES : 2 * LANES] + out[:, 2 * LANES : 3 * LANES]
    return summed, out[:, 3 * LANES :]


def backward_kernel(
    gauge_ref, top_ref, bot_ref, pass_ref, wet_ref, sv_ref, u1_ref, v1_ref, s2_ref, u2_ref, v2_ref,
    y_ref, yh_ref, t2_ref, kk_ref, t0_ref,
    grad_ref,
    x2p, x2r, pup, pvp, pvr, x1p, x1r, b2s, au1, av1, vs, ms, vt, mt, da, db, dc, dd,
):
    total = s2_ref.shape[0]
    tiles = total // ROWS
    lane, sub = masks(ROWS * STEP)
    dlane = lax.broadcasted_iota(jnp.int32, (tiles, LANES), 1)
    clear_ends(x2p, pup, pvp, x1p, da, db, dc, dd)
    blocks = range(0, tiles, STEP)

    def cut(c, lead=0):
        return slice(lead + ROWS * c, lead + ROWS * (c + STEP))

    x = gauge_ref[...]
    turned = jnp.concatenate([x, pltpu.roll(x, LANES - 4, 1)], axis=0)
    if turned.shape[0] < LANES:
        fill = jnp.full((LANES - turned.shape[0], LANES), -1.0, jnp.float32)
        turned = jnp.concatenate([turned, fill], axis=0)
    turned = jnp.transpose(turned)
    for group in range(3):
        places, lanes, values = [], [], []
        for k in range(4):
            cell = turned[8 * group + k : 8 * group + k + 1, :].astype(jnp.int32)
            value = turned[64 + 8 * group + k : 65 + 8 * group + k, :]
            row, col = cell >> 13, cell & 8191
            tile = col >> 7
            if group == 0:
                place = jnp.where(cell < 0, -1, tile * ROWS + row)
            elif group == 1:
                place = jnp.where((cell < 0) | (row < 5), -1, (7 - row) * tiles + tile)
            else:
                place = jnp.where((cell < 0) | (row > 2), -1, row * tiles + tile)
            places.append(place)
            lanes.append(col & 127)
            values.append(value)
        if group == 0:
            vs[...], ms[...] = gauge_fields(places, lanes, values, total)
        else:
            first = (group - 1) * 3 * tiles
            sums, counts = gauge_fields(places, lanes, values, 3 * tiles)
            vt[first : first + 3 * tiles, :] = sums
            mt[first : first + 3 * tiles, :] = counts
    sides = ((top_ref, -1.0, 0, (da, db)), (bot_ref, 1.0, ROWS - 1, (dc, dd)))

    def got(ref, n, name):
        place = SLOT[(n, name)]
        return ref[place * tiles : (place + 1) * tiles, :]

    kept = []
    for d, (ref, sigma, edge, scr) in enumerate(sides):
        values = [pass_ref[(d * len(PASS) + i) * tiles : (d * len(PASS) + i + 1) * tiles, :] for i in range(len(PASS))]
        senses = []
        for n in (1, 2, 3):
            first = (d * 3 + n - 1) * tiles
            count, summed = mt[first : first + tiles, :], vt[first : first + tiles, :]
            senses.append((1.0 + count) * values[n - 1] - got(ref, n, "sv") - summed)
        x2_1 = jnp.where(got(ref, 1, "r") > 0.0, senses[0], 0.0)
        x2_2 = jnp.where(got(ref, 2, "h") > 0.0, senses[1], 0.0)
        x2_3 = jnp.where(got(ref, 3, "h") > 0.0, senses[2], 0.0)
        x2r[pl.ds(edge, tiles, stride=ROWS), :] = x2_1
        y1, w0_1 = values[3], values[4]
        pu_1 = 0.25 * y1 * across_dense(x2_1, scr[0], dlane)
        pv_2 = (0.25 * sigma) * got(ref, 2, "h") * (x2_3 - x2_1)
        kept.append((senses[0] + across_dense(pu_1, scr[1], dlane) + sigma * pv_2, x2_2, y1, w0_1))
    for c in blocks:
        at = cut(c)
        wet = wet_ref[cut(c, total), :].astype(jnp.float32)
        b2 = (1.0 + ms[at, :]) * s2_ref[at, :] - sv_ref[at, :] - vs[at, :]
        b2s[at, :] = b2
        x2p[cut(c, ROWS), :] = wet * b2
    for (ref, sigma, edge, scr), (part, x2_2, y1, w0_1) in zip(sides, kept):
        pvr[pl.ds(edge, tiles, stride=ROWS), :] = (0.25 * sigma) * y1 * (x2_2 - row_of(x2p, edge, tiles, ROWS))
    for c in blocks:
        at = cut(c)
        a_u2 = 0.25 * across(x2p, c, STEP, lane)
        a_v2 = 0.25 * along(x2p, x2r, c, STEP, sub)
        energy = a_u2 * u2_ref[at, :] + a_v2 * v2_ref[at, :]
        y, yh, pull = y_ref[at, :], yh_ref[at, :], energy * kk_ref[at, :]
        pup[cut(c, ROWS), :] = yh * a_u2
        pvp[cut(c, ROWS), :] = yh * a_v2
        au1[at, :] = y * a_u2 - pull * u1_ref[at, :]
        av1[at, :] = y * a_v2 - pull * v1_ref[at, :]
        vs[at, :] = energy * t2_ref[at, :]
    for (ref, sigma, edge, scr), (part, x2_2, y1, w0_1) in zip(sides, kept):
        x1r[pl.ds(edge, tiles, stride=ROWS), :] = w0_1 * (part - sigma * row_of(pvp, edge, tiles, ROWS))
    for c in blocks:
        at = cut(c)
        wet = wet_ref[at, :].astype(jnp.float32)
        a_s1 = b2s[at, :] + across(pup, c, STEP, lane) + along(pvp, pvr, c, STEP, sub)
        x1p[cut(c, ROWS), :] = wet * a_s1
    for c in blocks:
        at = cut(c)
        a_u1 = au1[at, :] + 0.25 * across(x1p, c, STEP, lane)
        a_v1 = av1[at, :] + 0.25 * along(x1p, x1r, c, STEP, sub)
        energy = a_u1 * u1_ref[at, :] + a_v1 * v1_ref[at, :]
        grad_ref[at, :] = -(energy * t0_ref[at, :] + vs[at, :])


def gauge_kernel(tile_ref, cell_ref, value_ref, out_ref):
    strips = out_ref.shape[0]
    listed = tile_ref.shape[1]
    hit = lax.broadcasted_iota(jnp.int32, (strips, listed), 0) == tile_ref[...]
    earlier = lax.broadcasted_iota(jnp.int32, (listed, listed), 0) < lax.broadcasted_iota(jnp.int32, (listed, listed), 1)
    rank = jnp.dot(
        jnp.where(hit, 1.0, 0.0).astype(jnp.bfloat16), jnp.where(earlier, 1.0, 0.0).astype(jnp.bfloat16),
        preferred_element_type=jnp.float32,
    )
    rank = jnp.where(hit, rank, -1.0)
    cell = cell_ref[...].astype(jnp.float32) + 1.0
    value = value_ref[...]
    lane = lax.broadcasted_iota(jnp.int32, (strips, LANES), 1)
    line = lax.broadcasted_iota(jnp.int32, (strips, LANES), 0)
    own = jnp.full((strips, LANES), -1.0, jnp.float32)
    for k in range(8):
        taken = rank == float(k)
        cells = jnp.sum(jnp.where(taken, cell, 0.0), axis=1, keepdims=True) - 1.0
        values = jnp.sum(jnp.where(taken, value, 0.0), axis=1, keepdims=True)
        own = jnp.where(lane == k, cells, jnp.where(lane == 64 + k, values, own))
    above = jnp.where(line == 0, -1.0, pltpu.roll(own, 1, 0))
    below = jnp.where(line == strips - 1, -1.0, pltpu.roll(own, strips - 1, 0))
    part = lane & 63
    out_ref[...] = jnp.where(part < 8, own, jnp.where(part < 16, pltpu.roll(above, 8, 1), pltpu.roll(below, 16, 1)))


def sum_kernel(x_ref, out_ref):
    count, lines = x_ref.shape[0], x_ref.shape[1]
    for k in range(lines // ROWS):
        acc = x_ref[0, ROWS * k : ROWS * (k + 1), :]
        for e in range(1, count):
            acc = acc + x_ref[e, ROWS * k : ROWS * (k + 1), :]
        out_ref[:, LANES * k : LANES * (k + 1)] = acc


def call(kernel, outs, scratch, name):
    shapes = [jax.ShapeDtypeStruct(o, jnp.float32) for o in outs]
    return pl.pallas_call(
        kernel,
        out_shape=shapes if len(shapes) > 1 else shapes[0],
        scratch_shapes=[pltpu.VMEM(s, jnp.float32) for s in scratch],
        name=name,
        compiler_params=pltpu.CompilerParams(vmem_limit_bytes=48 * 1024 * 1024),
    )


def tiled(field):
    rows, cols = field.shape[-2:]
    lead = field.shape[:-2]
    parts = field.reshape(-1, rows, cols // LANES, LANES)
    return jnp.transpose(parts, (0, 2, 1, 3)).reshape(-1, LANES)


def shifted(value, axis, steps):
    count = lax.axis_size(axis)
    initial, last = max(0, -steps), min(count, count - steps)
    return lax.ppermute(value, axis, [(i, i + steps) for i in range(initial, last)])


def per_device(s0, u0, v0, depth, rough, wet, gauge_tiles, gauge_cells, gauge_values, survey):
    row_count, col_count = depth.shape
    assert row_count == ROWS and col_count == 8192
    total = row_count * col_count // LANES
    tiles = col_count // LANES
    strips = lax.axis_size("tile")
    events = lax.axis_size("event")
    s0, u0, v0, depth, rough, wet, survey = (tiled(f) for f in (s0[0], u0[0], v0[0], depth, rough, wet[0], survey[0]))
    field, padded, dense = (total, LANES), (total + 2 * ROWS, LANES), (tiles + 2 * ROWS, LANES)
    packet = (len(SENT) * tiles, LANES)
    down, up, u1, v1i, b, q1, k, t0, kr = call(
        prepare_kernel, [packet, packet] + [field] * 7, [padded] * 6 + [field] * 4, "prepare"
    )(s0, u0, v0, depth, rough, wet, survey)
    from_above = shifted(down, "tile", 1)
    from_below = shifted(up, "tile", -1)
    listed = gauge_cells.shape[1]
    send = call(gauge_kernel, [(strips, LANES)], [], "gauges")(
        gauge_tiles.reshape(1, listed), gauge_cells.reshape(1, listed), gauge_values.reshape(1, listed)
    )
    gauges = lax.all_to_all(send, "tile", 0, 0, tiled=True)
    rim_pass = (2 * len(PASS) * tiles, LANES)
    v1, s2, u2, v2, y, yh, t2, kk, passed = call(
        forward_kernel, [field] * 8 + [rim_pass], [padded] * 4 + [field] * 3 + [dense] * 6, "forward"
    )(from_above, from_below, s0, depth, wet, u1, v1i, b, q1, k, kr)
    grad = call(
        backward_kernel, [field],
        [padded, field, padded, padded, field, padded, field, field, field, field, field, field]
        + [(6 * tiles, LANES)] * 2 + [dense] * 4,
        "backward",
    )(gauges, from_above, from_below, passed, wet, survey, u1, v1, s2, u2, v2, y, yh, t2, kk, t0)
    parts = lax.all_to_all(grad.reshape(events, total // events, LANES), "event", 0, 0, tiled=True)
    return call(sum_kernel, [(ROWS, col_count // events)], [], "total")(parts)


def solution(mesh):
    placed = (
        P("event", "tile", None),
        P("event", "tile", None),
        P("event", "tile", None),
        P("tile", None),
        P("tile", None),
        P("event", None, "tile", None),
        P("event", "tile", None),
        P("event", "tile"),
        P("event", "tile"),
        P("event", "tile", None),
    )
    return jax.shard_map(
        per_device, mesh=mesh, in_specs=placed, out_specs=P("tile", "event"), check_vma=False
    )
```

time: 218 us -> 76.5 us (0.35)
  the two profiles are of different devices: /device:TPU:2 before, /device:TPU:1 now
where the time goes in v1:
time: 76.5 us; the launch traced here: 75.6 us
  local copies, waits for them, and re-layouts  28.2 us (37%)
  starting transfers between devices  25.7 us (34%)
  blocking collectives  13.3 us (17%)
  Pallas kernels  6.22 us (8%)
  waiting for transfers between devices  1.93 us (3%)
    unnamed x80, local copies, waits for them, and re-layouts  28.2 us
    all_to_all x1, starting transfers between devices, per_device(): gauges = lax.all_to_all(send, 'tile', 0, 0, tiled=True)  19.9 us
    all_to_all x1, blocking collectives, per_device(): lax.all_to_all(grad.reshape(events, total // events, LANES), 'event', 0,...  13.3 us
    ppermute x2, starting transfers between devices, shifted(): lax.ppermute(value, axis, [(i, i + steps) for i in range(initial, last)])  5.81 us
    pallas_call x1, Pallas kernels, per_device(): call(prepare_kernel, [packet, packet] + [field] * 7, [padded] * 6 + [fiel...  2.17 us
    all_to_all x1, waiting for transfers between devices, per_device(): gauges = lax.all_to_all(send, 'tile', 0, 0, tiled=True)  1.92 us
  transfers between devices with their start and end apart: 3, of which 1 were waited for; matrix products, arithmetic and copies ran while one was open for 0% of the time, Pallas kernels for 3%

profile of v1, /device:TPU:1, one launch (start us, length us, event | category | flops | bytes accessed | tf_op | source)
XLA Modules:
  0.0 75.6 jit_solution(10519124591646447680)
XLA Ops:
  0.0 1.0 %copy-done = s32[1,2,8,8192]{3,2,1,0:T(8,128)S(1)} copy-done((s32[1,2,8,8192]{3,2,1,0:T(8,128)S(1)}, s32[1,2,8,8192]{3,2,1,0:T(8,128)}, u32[]{:S(2)}) %copy-start) | copy-done | bytes 524312
  1.0 0.9 %copy-done.2 = f32[1,8,8192]{2,1,0:T(8,128)S(1)} copy-done((f32[1,8,8192]{2,1,0:T(8,128)S(1)}, f32[1,8,8192]{2,1,0:T(8,128)}, u32[]{:S(2)}) %copy-start.2) | copy-done | bytes 262168
  2.0 0.9 %copy-done.4 = f32[1,8,8192]{2,1,0:T(8,128)S(1)} copy-done((f32[1,8,8192]{2,1,0:T(8,128)S(1)}, f32[1,8,8192]{2,1,0:T(8,128)}, u32[]{:S(2)}) %copy-start.4) | copy-done | bytes 262168
  2.9 0.9 %copy-done.6 = f32[8,8192]{1,0:T(8,128)S(1)} copy-done((f32[8,8192]{1,0:T(8,128)S(1)}, f32[8,8192]{1,0:T(8,128)}, u32[]{:S(2)}) %copy-start.6) | copy-done | bytes 262168
  3.9 0.9 %copy-done.24 = f32[1,8,8192]{2,1,0:T(8,128)S(1)} copy-done((f32[1,8,8192]{2,1,0:T(8,128)S(1)}, f32[1,8,8192]{2,1,0:T(8,128)}, u32[]{:S(2)}) %copy-start.24) | copy-done | bytes 262168
  4.8 0.9 %copy-done.25 = f32[1,8,8192]{2,1,0:T(8,128)S(1)} copy-done((f32[1,8,8192]{2,1,0:T(8,128)S(1)}, f32[1,8,8192]{2,1,0:T(8,128)}, u32[]{:S(2)}) %copy-start.25) | copy-done | bytes 262168
  5.8 0.9 %copy-done.26 = f32[8,8192]{1,0:T(8,128)S(1)} copy-done((f32[8,8192]{1,0:T(8,128)S(1)}, f32[8,8192]{1,0:T(8,128)}, u32[]{:S(2)}) %copy-start.26) | copy-done | bytes 262168
  6.8 2.2 %prepare.1 = (f32[1152,128]{1,0:T(8,128)}, f32[1152,128]{1,0:T(8,128)}, f32[512,128]{1,0:T(8,128)S(1)}, f32[512,128]{1,0:T(8,128)S(1)}, f32[512,128]{1,0:T(8,128...) custom-call(f32[512,128]{1,0:T(8,128)S(1)} %bitcast.47, ...), custom_call_target="tpu_custom_call" | custom-call | tf_op jit(solution)/shard_map/prepare/pallas_call | solution.py:421
  12.4 4.4 %collective-permute-start = (f32[1152,128]{1,0:T(8,128)}, f32[1152,128]{1,0:T(8,128)S(1)}, u32[]{:S(2)}, u32[]{:S(2)}) collective-permute-start(f32[1152,128]{1,0:T(8,128)} %get-tuple-element.23), channel_id=1, source_target_pairs={{0,1},{1,2},{2,3},{3,4},{4,5},{5,6},{6,7},{7,8},{8,9},{9,10},{10,1... | collective-permute-start | bytes 1769480 | tf_op jit(solution)/shard_map/ppermute | solution.py:408
  16.9 1.4 %collective-permute-start.1 = (f32[1152,128]{1,0:T(8,128)}, f32[1152,128]{1,0:T(8,128)S(1)}, u32[]{:S(2)}, u32[]{:S(2)}) collective-permute-start(f32[1152,128]{1,0:T(8,128)} %get-tuple-element.24), channel_id=1, source_target_pairs={{1,0},{2,1},{3,2},{4,3},{5,4},{6,5},{7,6},{8,7},{9,8},{10,9},{11,1... | collective-permute-start | bytes 1769480 | tf_op jit(solution)/shard_map/ppermute | solution.py:408
  18.3 1.1 %gauges.1 = f32[64,128]{1,0:T(8,128)} custom-call(s32[1,256]{1,0:T(1,128)S(1)} %bitcast.55, s32[1,256]{1,0:T(1,128)S(1)} %copy-done.38, f32[1,256]{1,0:T(1,128)S(1)} %copy-done.39), custom_call_target="tpu_custom_call" | custom-call | tf_op jit(solution)/shard_map/gauges/pallas_call | solution.py:427
  19.4 19.9 %all-to-all-start = ((f32[64,1,128]{2,1,0:T(1,128)}), f32[64,1,128]{2,1,0:T(1,128)S(1)}, u32[]{:S(2)}, u32[]{:S(2)}) async-start(f32[64,1,128]{2,1,0:T(1,128)} %bitcast.2), calls=%async_computation | async-start | bytes 65536 | tf_op jit(solution)/shard_map/all_to_all | solution.py:430
  39.4 0.9 %copy-done.28 = f32[512,128]{1,0:T(8,128)S(1)} copy-done((f32[512,128]{1,0:T(8,128)S(1)}, f32[512,128]{1,0:T(8,128)}, u32[]{:S(2)}) %copy-start.28) | copy-done | bytes 262168
  40.3 0.9 %copy-done.30 = f32[512,128]{1,0:T(8,128)S(1)} copy-done((f32[512,128]{1,0:T(8,128)S(1)}, f32[512,128]{1,0:T(8,128)}, u32[]{:S(2)}) %copy-start.30) | copy-done | bytes 262168
  41.3 0.9 %copy-done.32 = f32[512,128]{1,0:T(8,128)S(1)} copy-done((f32[512,128]{1,0:T(8,128)S(1)}, f32[512,128]{1,0:T(8,128)}, u32[]{:S(2)}) %copy-start.32) | copy-done | bytes 262168
  42.2 0.9 %copy-done.34 = f32[512,128]{1,0:T(8,128)S(1)} copy-done((f32[512,128]{1,0:T(8,128)S(1)}, f32[512,128]{1,0:T(8,128)}, u32[]{:S(2)}) %copy-start.34) | copy-done | bytes 262168
  43.2 0.9 %copy-done.36 = f32[512,128]{1,0:T(8,128)S(1)} copy-done((f32[512,128]{1,0:T(8,128)S(1)}, f32[512,128]{1,0:T(8,128)}, u32[]{:S(2)}) %copy-start.36) | copy-done | bytes 262168
  44.1 0.9 %forward.1 = (f32[512,128]{1,0:T(8,128)S(1)}, f32[512,128]{1,0:T(8,128)S(1)}, f32[512,128]{1,0:T(8,128)S(1)}, f32[512,128]{1,0:T(8,128)S(1)}, f32[512,128]{1,0:T...) custom-call(f32[1152,128]{1,0:T(8,128)S(1)} %collective-permute-done, ...), custom_call_target="tpu_custom_call" | custom-call | tf_op jit(solution)/shard_map/forward/pallas_call | solution.py:432
  45.7 0.7 copy-done.10
  46.4 0.7 copy-done.12
  48.6 0.7 copy-done.18
  50.7 1.9 %all-to-all-done = f32[64,1,128]{2,1,0:T(1,128)S(1)} async-done(((f32[64,1,128]{2,1,0:T(1,128)}), f32[64,1,128]{2,1,0:T(1,128)S(1)}, u32[]{:S(2)}, u32[]{:S(2)}) %all-to-all-start) | async-done | bytes 32800 | tf_op jit(solution)/shard_map/all_to_all | solution.py:430
  52.6 0.9 %copy-done.9 = f32[512,128]{1,0:T(8,128)S(1)} copy-done((f32[512,128]{1,0:T(8,128)S(1)}, f32[512,128]{1,0:T(8,128)}, u32[]{:S(2)}) %copy-start.9) | copy-done | bytes 262168
  53.5 0.9 %copy-done.11 = f32[512,128]{1,0:T(8,128)S(1)} copy-done((f32[512,128]{1,0:T(8,128)S(1)}, f32[512,128]{1,0:T(8,128)}, u32[]{:S(2)}) %copy-start.11) | copy-done | bytes 262168
  54.5 0.9 %copy-done.13 = f32[512,128]{1,0:T(8,128)S(1)} copy-done((f32[512,128]{1,0:T(8,128)S(1)}, f32[512,128]{1,0:T(8,128)}, u32[]{:S(2)}) %copy-start.13) | copy-done | bytes 262168
  55.4 0.9 %copy-done.15 = f32[512,128]{1,0:T(8,128)S(1)} copy-done((f32[512,128]{1,0:T(8,128)S(1)}, f32[512,128]{1,0:T(8,128)}, u32[]{:S(2)}) %copy-start.15) | copy-done | bytes 262168
  56.4 0.9 %copy-done.17 = f32[512,128]{1,0:T(8,128)S(1)} copy-done((f32[512,128]{1,0:T(8,128)S(1)}, f32[512,128]{1,0:T(8,128)}, u32[]{:S(2)}) %copy-start.17) | copy-done | bytes 262168
  57.3 0.9 %copy-done.19 = f32[512,128]{1,0:T(8,128)S(1)} copy-done((f32[512,128]{1,0:T(8,128)S(1)}, f32[512,128]{1,0:T(8,128)}, u32[]{:S(2)}) %copy-start.19) | copy-done | bytes 262168
  58.3 0.9 %copy-done.21 = f32[512,128]{1,0:T(8,128)S(1)} copy-done((f32[512,128]{1,0:T(8,128)S(1)}, f32[512,128]{1,0:T(8,128)}, u32[]{:S(2)}) %copy-start.21) | copy-done | bytes 262168
  59.2 0.9 %copy-done.23 = f32[512,128]{1,0:T(8,128)S(1)} copy-done((f32[512,128]{1,0:T(8,128)S(1)}, f32[512,128]{1,0:T(8,128)}, u32[]{:S(2)}) %copy-start.23) | copy-done | bytes 262168
  60.2 1.4 %backward.1 = f32[512,128]{1,0:T(8,128)S(1)} custom-call(f32[64,128]{1,0:T(8,128)S(1)} %bitcast.54, f32[1152,128]{1,0:T(8,128)S(1)} %collective-permute-done.top_ref, f32[1152,128]{1,0:T(8,128)S(1)} %collective-permute-done.1.bot_ref, f32[640,128]{1,0:T(8,128)S(1)} %get-tuple-element.31.pass_ref, s32[1024,128]{1,0:T(8,128)S(1)} %bitcast.43, ...), custom_call_target="tpu_custom_call" | custom-call | tf_op jit(solution)/shard_map/backward/pallas_call | solution.py:435
  61.6 13.3 %all_to_all.16.x_ref = f32[8,64,128]{2,1,0:T(8,128)S(1)} all-to-all(f32[8,64,128]{2,1,0:T(8,128)S(1)} %bitcast.44), channel_id=1, replica_groups=mesh['event'=8,'tile'=64] {'event'}, dimensions={0} | all-to-all | bytes 524288 | tf_op jit(solution)/shard_map/all_to_all | solution.py:441
  (60 shorter events, 7.7 us)
Async XLA Ops:
  0.0 1.0 %copy-start = (s32[1,2,8,8192]{3,2,1,0:T(8,128)S(1)}, s32[1,2,8,8192]{3,2,1,0:T(8,128)}, u32[]{:S(2)}) copy-start(s32[1,2,8,8192]{3,2,1,0:T(8,128)} %param.15) | copy-start | bytes 1572868
  1.0 0.9 %copy-start.2 = (f32[1,8,8192]{2,1,0:T(8,128)S(1)}, f32[1,8,8192]{2,1,0:T(8,128)}, u32[]{:S(2)}) copy-start(f32[1,8,8192]{2,1,0:T(8,128)} %param.19) | copy-start | bytes 786436
  2.0 0.9 %copy-start.4 = (f32[1,8,8192]{2,1,0:T(8,128)S(1)}, f32[1,8,8192]{2,1,0:T(8,128)}, u32[]{:S(2)}) copy-start(f32[1,8,8192]{2,1,0:T(8,128)} %param.10) | copy-start | bytes 786436
  2.9 0.9 %copy-start.6 = (f32[8,8192]{1,0:T(8,128)S(1)}, f32[8,8192]{1,0:T(8,128)}, u32[]{:S(2)}) copy-start(f32[8,8192]{1,0:T(8,128)} %param.13) | copy-start | bytes 786436
  3.9 0.9 %copy-start.24 = (f32[1,8,8192]{2,1,0:T(8,128)S(1)}, f32[1,8,8192]{2,1,0:T(8,128)}, u32[]{:S(2)}) copy-start(f32[1,8,8192]{2,1,0:T(8,128)} %param.11) | copy-start | bytes 786436
  4.8 0.9 %copy-start.25 = (f32[1,8,8192]{2,1,0:T(8,128)S(1)}, f32[1,8,8192]{2,1,0:T(8,128)}, u32[]{:S(2)}) copy-start(f32[1,8,8192]{2,1,0:T(8,128)} %param.12) | copy-start | bytes 786436
  5.8 0.9 %copy-start.26 = (f32[8,8192]{1,0:T(8,128)S(1)}, f32[8,8192]{1,0:T(8,128)}, u32[]{:S(2)}) copy-start(f32[8,8192]{1,0:T(8,128)} %param.14) | copy-start | bytes 786436
  6.7 32.6 %copy-start.1 = (s32[1,2,8,8192]{3,2,1,0:T(8,128)S(1)}, s32[1,2,8,8192]{3,2,1,0:T(8,128)}, u32[]{:S(2)}) copy-start(s32[1,2,8,8192]{3,2,1,0:T(8,128)} %param.15) | copy-start | bytes 1572868
  6.7 32.6 %copy-start.5 = (f32[1,8,8192]{2,1,0:T(8,128)S(1)}, f32[1,8,8192]{2,1,0:T(8,128)}, u32[]{:S(2)}) copy-start(f32[1,8,8192]{2,1,0:T(8,128)} %param.10) | copy-start | bytes 786436
  6.8 32.6 %copy-start.7 = (f32[8,8192]{1,0:T(8,128)S(1)}, f32[8,8192]{1,0:T(8,128)}, u32[]{:S(2)}) copy-start(f32[8,8192]{1,0:T(8,128)} %param.13) | copy-start | bytes 786436
  12.4 26.9 %collective-permute-start = (f32[1152,128]{1,0:T(8,128)}, f32[1152,128]{1,0:T(8,128)S(1)}, u32[]{:S(2)}, u32[]{:S(2)}) collective-permute-start(f32[1152,128]{1,0:T(8,128)} %get-tuple-element.23), channel_id=1, source_target_pairs={{0,1},{1,2},{2,3},{3,4},{4,5},{5,6},{6,7},{7,8},{8,9},{9,10},{10,1... | collective-permute-start | bytes 1769480 | tf_op jit(solution)/shard_map/ppermute | solution.py:408
  16.8 1.5 %copy-start.38 = (s32[1,256]{1,0:T(1,128)S(1)}, s32[1,256]{1,0:T(1,128)}, u32[]{:S(2)}) copy-start(s32[1,256]{1,0:T(1,128)} %cell_ref.1) | copy-start | bytes 3076
  16.8 1.5 %copy-start.39 = (f32[1,256]{1,0:T(1,128)S(1)}, f32[1,256]{1,0:T(1,128)}, u32[]{:S(2)}) copy-start(f32[1,256]{1,0:T(1,128)} %value_ref.1) | copy-start | bytes 3076
  16.8 1.5 %copy-start.37 = (s32[1,256,1]{1,2,0:T(1,128)S(1)}, s32[1,256,1]{1,2,0:T(1,128)}, u32[]{:S(2)}) copy-start(s32[1,256,1]{1,2,0:T(1,128)} %param.16) | copy-start | bytes 3076
  16.9 22.4 %collective-permute-start.1 = (f32[1152,128]{1,0:T(8,128)}, f32[1152,128]{1,0:T(8,128)S(1)}, u32[]{:S(2)}, u32[]{:S(2)}) collective-permute-start(f32[1152,128]{1,0:T(8,128)} %get-tuple-element.24), channel_id=1, source_target_pairs={{1,0},{2,1},{3,2},{4,3},{5,4},{6,5},{7,6},{8,7},{9,8},{10,9},{11,1... | collective-permute-start | bytes 1769480 | tf_op jit(solution)/shard_map/ppermute | solution.py:408
  19.4 33.2 %all-to-all-start = ((f32[64,1,128]{2,1,0:T(1,128)}), f32[64,1,128]{2,1,0:T(1,128)S(1)}, u32[]{:S(2)}, u32[]{:S(2)}) async-start(f32[64,1,128]{2,1,0:T(1,128)} %bitcast.2), calls=%async_computation | async-start | bytes 65536 | tf_op jit(solution)/shard_map/all_to_all | solution.py:430
  39.3 1.0 %copy-start.28 = (f32[512,128]{1,0:T(8,128)S(1)}, f32[512,128]{1,0:T(8,128)}, u32[]{:S(2)}) copy-start(f32[512,128]{1,0:T(8,128)} %copy-done.27) | copy-start | bytes 786436
  40.3 0.9 %copy-start.30 = (f32[512,128]{1,0:T(8,128)S(1)}, f32[512,128]{1,0:T(8,128)}, u32[]{:S(2)}) copy-start(f32[512,128]{1,0:T(8,128)} %copy-done.29) | copy-start | bytes 786436
  41.2 0.9 %copy-start.32 = (f32[512,128]{1,0:T(8,128)S(1)}, f32[512,128]{1,0:T(8,128)}, u32[]{:S(2)}) copy-start(f32[512,128]{1,0:T(8,128)} %copy-done.31) | copy-start | bytes 786436
  42.2 0.9 %copy-start.34 = (f32[512,128]{1,0:T(8,128)S(1)}, f32[512,128]{1,0:T(8,128)}, u32[]{:S(2)}) copy-start(f32[512,128]{1,0:T(8,128)} %copy-done.33) | copy-start | bytes 786436
  43.1 0.9 %copy-start.36 = (f32[512,128]{1,0:T(8,128)S(1)}, f32[512,128]{1,0:T(8,128)}, u32[]{:S(2)}) copy-start(f32[512,128]{1,0:T(8,128)} %copy-done.35) | copy-start | bytes 786436
  44.1 8.5 %copy-start.3 = (f32[1,8,8192]{2,1,0:T(8,128)S(1)}, f32[1,8,8192]{2,1,0:T(8,128)}, u32[]{:S(2)}) copy-start(f32[1,8,8192]{2,1,0:T(8,128)} %param.19) | copy-start | bytes 786436
  46.4 0.7 copy-start.12
  48.6 0.7 copy-start.18
  52.6 1.0 %copy-start.9 = (f32[512,128]{1,0:T(8,128)S(1)}, f32[512,128]{1,0:T(8,128)}, u32[]{:S(2)}) copy-start(f32[512,128]{1,0:T(8,128)} %copy-done.8) | copy-start | bytes 786436
  53.5 0.9 %copy-start.11 = (f32[512,128]{1,0:T(8,128)S(1)}, f32[512,128]{1,0:T(8,128)}, u32[]{:S(2)}) copy-start(f32[512,128]{1,0:T(8,128)} %copy-done.10) | copy-start | bytes 786436
  54.5 0.9 %copy-start.13 = (f32[512,128]{1,0:T(8,128)S(1)}, f32[512,128]{1,0:T(8,128)}, u32[]{:S(2)}) copy-start(f32[512,128]{1,0:T(8,128)} %copy-done.12) | copy-start | bytes 786436
  55.4 0.9 %copy-start.15 = (f32[512,128]{1,0:T(8,128)S(1)}, f32[512,128]{1,0:T(8,128)}, u32[]{:S(2)}) copy-start(f32[512,128]{1,0:T(8,128)} %copy-done.14) | copy-start | bytes 786436
  56.4 0.9 %copy-start.17 = (f32[512,128]{1,0:T(8,128)S(1)}, f32[512,128]{1,0:T(8,128)}, u32[]{:S(2)}) copy-start(f32[512,128]{1,0:T(8,128)} %copy-done.16) | copy-start | bytes 786436
  57.3 0.9 %copy-start.19 = (f32[512,128]{1,0:T(8,128)S(1)}, f32[512,128]{1,0:T(8,128)}, u32[]{:S(2)}) copy-start(f32[512,128]{1,0:T(8,128)} %copy-done.18) | copy-start | bytes 786436
  58.3 0.9 %copy-start.21 = (f32[512,128]{1,0:T(8,128)S(1)}, f32[512,128]{1,0:T(8,128)}, u32[]{:S(2)}) copy-start(f32[512,128]{1,0:T(8,128)} %copy-done.20) | copy-start | bytes 786436
  59.2 0.9 %copy-start.23 = (f32[512,128]{1,0:T(8,128)S(1)}, f32[512,128]{1,0:T(8,128)}, u32[]{:S(2)}) copy-start(f32[512,128]{1,0:T(8,128)} %copy-done.22) | copy-start | bytes 786436
  (11 other events, 7.7 us)

commit v2 on v1

--- a/solution.py
+++ b/solution.py
@@ -9,12 +9,15 @@
 LANES = 128
 ROWS = 8
 STEP = 4
+GRANT = 16 * 1024 * 1024
+HERE = None
 RIM1 = ("s0", "v1", "b", "s1", "r", "u1", "k", "sv")
 RIM2 = ("s1", "w0", "v2", "h", "u2", "sv")
 RIM3 = ("v2", "h", "s2", "sv")
 SENT = tuple((1, x) for x in RIM1) + tuple((2, x) for x in RIM2) + tuple((3, x) for x in RIM3)
 SLOT = {key: i for i, key in enumerate(SENT)}
-PASS = ("s2_1", "s2_2", "s2_3", "y1", "w0")
+PASS = ("s2_1", "s2_2", "s2_3", "y1", "w0", "h2", "h3", "sv1", "sv2", "sv3")
+EDGES = ((1, "s0"), (1, "v1"), (1, "b"))
 
 
 def masks(rows):
@@ -61,15 +64,17 @@
 
 
 def prepare_kernel(
-    s0_ref, u0_ref, v0_ref, h_ref, rough_ref, wet_ref, sv_ref,
-    down_ref, up_ref, u1_ref, v1_ref, b_ref, q1_ref, k_ref, t0_ref, kr_ref,
-    s0p, u1p, v1p, s1p, u2p, v2p, hh, rr, w0q, s2p,
+    tile_ref, cell_ref, value_ref, s0p, h_ref, rough_ref, u0_ref, v0_ref, wet_ref, sv_ref,
+    down_ref, up_ref, send_ref, edge_ref, u1_ref, v1_ref, q1_ref, k_ref, t0_ref, kr_ref,
+    u1p, v1p, s1p, u2p, v2p, hh, s2p, b_ref, w0q, w1_ref, rr, *, arrive, leave,
 ):
-    total = s0_ref.shape[0]
+    total = u1_ref.shape[0]
     tiles = total // ROWS
     lane, sub = masks(ROWS * STEP)
     clear_ends(s0p, u1p, v1p, s1p, u2p, v2p)
-    s0p[ROWS : ROWS + total, :] = s0_ref[...]
+    arrive(0, 1, 2)
+    gauge_table(tile_ref, cell_ref, value_ref, send_ref)
+    arrive(3, 4, 5, 6, 7, 8)
     blocks = range(0, tiles, STEP)
 
     def cut(c, lead=0):
@@ -96,12 +101,14 @@
         kr_ref[at, :] = kr
         t0_ref[at, :] = kr * speed * inverse
         w0q[at, :] = 0.25 * wet
+    leave(4, 5, 7, 8, 9)
     for c in blocks:
         at = cut(c)
         quarter = w0q[at, :]
-        q1 = s0_ref[at, :] - quarter * across(u1p, c, STEP, lane)
+        q1 = s0p[cut(c, ROWS), :] - quarter * across(u1p, c, STEP, lane)
         q1_ref[at, :] = q1
         s1p[cut(c, ROWS), :] = q1 - quarter * along(v1p, None, c, STEP, sub)
+    leave(6)
     for c in blocks:
         at = cut(c)
         wet = wet_ref[cut(c, total), :].astype(jnp.float32)
@@ -111,20 +118,27 @@
         h = depth * y
         hh[at, :] = h
         rr[at, :] = depth * wet
+        w1_ref[at, :] = wet
         u2p[cut(c, ROWS), :] = y * east - h * across(s1p, c, STEP, lane)
         v2p[cut(c, ROWS), :] = y * north - h * along(s1p, None, c, STEP, sub)
     for c in blocks:
         at = cut(c)
-        wet = wet_ref[cut(c, total), :].astype(jnp.float32)
         change = across(u2p, c, STEP, lane) + along(v2p, None, c, STEP, sub)
-        s2p[at, :] = s1p[cut(c, ROWS), :] - 0.25 * wet * change
+        s2p[at, :] = s1p[cut(c, ROWS), :] - 0.25 * w1_ref[at, :] * change
     held = {
-        (1, "s0"): (s0_ref, 0), (1, "v1"): (v1_ref, 0), (1, "b"): (b_ref, 0), (1, "s1"): (s1p, ROWS),
+        (1, "s0"): (s0p, ROWS), (1, "v1"): (v1_ref, 0), (1, "b"): (b_ref, 0), (1, "s1"): (s1p, ROWS),
         (1, "r"): (rr, 0), (1, "u1"): (u1_ref, 0), (1, "k"): (k_ref, 0), (1, "sv"): (sv_ref, 0),
         (2, "s1"): (s1p, ROWS), (2, "w0"): (w0q, 0), (2, "v2"): (v2p, ROWS), (2, "h"): (hh, 0),
         (2, "u2"): (u2p, ROWS), (2, "sv"): (sv_ref, 0),
         (3, "v2"): (v2p, ROWS), (3, "h"): (hh, 0), (3, "s2"): (s2p, 0), (3, "sv"): (sv_ref, 0),
     }
+    arrive(9)
+    for i, key in enumerate(EDGES):
+        ref, lead = held[key]
+        for j, row in enumerate((0, ROWS - 1)):
+            first = (j * len(EDGES) + i) * tiles
+            edge_ref[first : first + tiles, :] = row_of(ref, row, tiles, lead)
+    leave(3)
     for key, place in SLOT.items():
         ref, lead = held[key]
         down_ref[place * tiles : (place + 1) * tiles, :] = row_of(ref, ROWS - key[0], tiles, lead)
@@ -132,11 +146,11 @@
 
 
 def forward_kernel(
-    top_ref, bot_ref, s0_ref, h_ref, wet_ref, u1_ref, v1i_ref, b_ref, q1_ref, k_ref, kr_ref,
+    edge_ref, top_ref, bot_ref, v1i_ref, q1_ref, wet_ref, u1_ref, k_ref, h_ref, kr_ref,
     v1_ref, s2_ref, u2_ref, v2_ref, y_ref, yh_ref, t2_ref, kk_ref, pass_ref,
-    v1p, s1p, u2p, v2p, v1r, s1r, v2r, da, db, dc, dd, de, df,
+    v1p, s1p, u2p, v2p, v1r, s1r, v2r, da, db, dc, dd, de, df, *, arrive, leave,
 ):
-    total = s0_ref.shape[0]
+    total = u1_ref.shape[0]
     tiles = total // ROWS
     lane, sub = masks(ROWS * STEP)
     dlane = lax.broadcasted_iota(jnp.int32, (tiles, LANES), 1)
@@ -152,13 +166,18 @@
         place = SLOT[(n, name)]
         return ref[place * tiles : (place + 1) * tiles, :]
 
+    def own(edge, i):
+        first = (len(EDGES) * (edge > 0) + i) * tiles
+        return edge_ref[first : first + tiles, :]
+
+    arrive(0, 3)
     v1p[ROWS : ROWS + total, :] = v1i_ref[...]
     kept = []
     for ref, sigma, edge, scr in sides:
         b = got(ref, 1, "b")
-        delta = b * row_of(s0_ref, edge, tiles)
+        delta = b * own(edge, 0)
         v1_1 = got(ref, 1, "v1") + sigma * delta
-        v1_e = row_of(v1i_ref, edge, tiles) - sigma * row_of(b_ref, edge, tiles) * got(ref, 1, "s0")
+        v1_e = own(edge, 1) - sigma * own(edge, 2) * got(ref, 1, "s0")
         v1p[pl.ds(ROWS + edge, tiles, stride=ROWS), :] = v1_e
         v1r[pl.ds(edge, tiles, stride=ROWS), :] = v1_1
         bump = got(ref, 2, "w0") * delta
@@ -176,11 +195,14 @@
         s2_3 = got(ref, 3, "s2") + (0.25 * sigma) * jnp.where(h3 > 0.0, 1.0, 0.0) * (v2_2 - v2i_2)
         u2_1 = (w1_1 * u1_1 - r * across_dense(s1_1, scr[1], dlane)) * inverse
         kept.append((v1_1, s1_1, s1_2, w0_1, w1_1, r, inverse, h2, v2_2, v2_3, u2_1, u2_2, s2_3))
+    arrive(4, 5)
     for c in blocks:
         at = cut(c)
         quarter = 0.25 * wet_ref[at, :].astype(jnp.float32)
         v1_ref[at, :] = v1p[cut(c, ROWS), :]
         s1p[cut(c, ROWS), :] = q1_ref[at, :] - quarter * along(v1p, v1r, c, STEP, sub)
+    leave(0)
+    arrive(6, 7, 8, 9)
     late = []
     for (ref, sigma, edge, scr), values in zip(sides, kept):
         v1_1, s1_1, s1_2, w0_1, w1_1, r, inverse, h2, v2_2, v2_3, u2_1, u2_2, s2_3 = values
@@ -192,14 +214,13 @@
         late.append((s2_2, across_dense(u2_1, scr[0], dlane)))
     for c in blocks:
         at = cut(c)
-        wet = wet_ref[cut(c, total), :].astype(jnp.float32)
         east, north = u1_ref[at, :], v1_ref[at, :]
         speed2 = east * east + north * north + 1.0
         slow = lax.rsqrt(speed2)
         speed = speed2 * slow
         k = k_ref[at, :]
         inverse = 1.0 / (1.0 + k * speed)
-        y = wet * inverse
+        y = wet_ref[cut(c, total), :].astype(jnp.float32) * inverse
         yh = 0.2 * h_ref[at, :] * y
         u2 = y * east - yh * across(s1p, c, STEP, lane)
         v2 = y * north - yh * along(s1p, s1r, c, STEP, sub)
@@ -211,19 +232,23 @@
         yh_ref[at, :] = yh
         t2_ref[at, :] = kr_ref[at, :] * speed * inverse
         kk_ref[at, :] = k * inverse * slow
+    leave(2, 3, 4, 5, 6, 7)
     for c in blocks:
         at = cut(c)
         wet = wet_ref[cut(c, total), :].astype(jnp.float32)
         change = across(u2p, c, STEP, lane) + along(v2p, v2r, c, STEP, sub)
         s2_ref[at, :] = s1p[cut(c, ROWS), :] - 0.25 * wet * change
+    leave(1)
     for d, ((ref, sigma, edge, scr), values, more) in enumerate(zip(sides, kept, late)):
         v1_1, s1_1, s1_2, w0_1, w1_1, r, inverse, h2, v2_2, v2_3, u2_1, u2_2, s2_3 = values
         s2_2, du2_1 = more
         v2_e = row_of(v2p, edge, tiles, ROWS)
         s2_1 = s1_1 - 0.25 * w1_1 * (du2_1 + sigma * (v2_2 - v2_e))
-        for i, value in enumerate((s2_1, s2_2, s2_3, r * inverse, w0_1)):
+        surveyed = [got(ref, n, "sv") for n in (1, 2, 3)]
+        for i, value in enumerate((s2_1, s2_2, s2_3, r * inverse, w0_1, h2, got(ref, 3, "h"), *surveyed)):
             first = (d * len(PASS) + i) * tiles
             pass_ref[first : first + tiles, :] = value
+    leave(8)
 
 
 def gauge_fields(places, lanes, values, rows):
@@ -249,10 +274,9 @@
 
 
 def backward_kernel(
-    gauge_ref, top_ref, bot_ref, pass_ref, wet_ref, sv_ref, u1_ref, v1_ref, s2_ref, u2_ref, v2_ref,
-    y_ref, yh_ref, t2_ref, kk_ref, t0_ref,
+    gauge_ref, s2_ref, sv_ref, wet_ref, pass_ref, u2_ref, v2_ref, kk_ref, y_ref, yh_ref, u1_ref, v1_ref, t2_ref, t0_ref,
     grad_ref,
-    x2p, x2r, pup, pvp, pvr, x1p, x1r, b2s, au1, av1, vs, ms, vt, mt, da, db, dc, dd,
+    x2p, x2r, pup, pvp, pvr, x1p, x1r, b2s, au1, av1, vs, ms, vt, mt, da, db, dc, dd, *, arrive, leave,
 ):
     total = s2_ref.shape[0]
     tiles = total // ROWS
@@ -293,35 +317,34 @@
             sums, counts = gauge_fields(places, lanes, values, 3 * tiles)
             vt[first : first + 3 * tiles, :] = sums
             mt[first : first + 3 * tiles, :] = counts
-    sides = ((top_ref, -1.0, 0, (da, db)), (bot_ref, 1.0, ROWS - 1, (dc, dd)))
-
-    def got(ref, n, name):
-        place = SLOT[(n, name)]
-        return ref[place * tiles : (place + 1) * tiles, :]
-
+    arrive(1, 2, 3, 4)
+    sides = ((-1.0, 0, (da, db)), (1.0, ROWS - 1, (dc, dd)))
     kept = []
-    for d, (ref, sigma, edge, scr) in enumerate(sides):
-        values = [pass_ref[(d * len(PASS) + i) * tiles : (d * len(PASS) + i + 1) * tiles, :] for i in range(len(PASS))]
+    for d, (sigma, edge, scr) in enumerate(sides):
+        got = {}
+        for i, name in enumerate(PASS):
+            first = (d * len(PASS) + i) * tiles
+            got[name] = pass_ref[first : first + tiles, :]
         senses = []
         for n in (1, 2, 3):
             first = (d * 3 + n - 1) * tiles
             count, summed = mt[first : first + tiles, :], vt[first : first + tiles, :]
-            senses.append((1.0 + count) * values[n - 1] - got(ref, n, "sv") - summed)
-        x2_1 = jnp.where(got(ref, 1, "r") > 0.0, senses[0], 0.0)
-        x2_2 = jnp.where(got(ref, 2, "h") > 0.0, senses[1], 0.0)
-        x2_3 = jnp.where(got(ref, 3, "h") > 0.0, senses[2], 0.0)
+            senses.append((1.0 + count) * got[f"s2_{n}"] - got[f"sv{n}"] - summed)
+        y1, h2 = got["y1"], got["h2"]
+        x2_1 = jnp.where(y1 > 0.0, senses[0], 0.0)
+        x2_2 = jnp.where(h2 > 0.0, senses[1], 0.0)
+        x2_3 = jnp.where(got["h3"] > 0.0, senses[2], 0.0)
         x2r[pl.ds(edge, tiles, stride=ROWS), :] = x2_1
-        y1, w0_1 = values[3], values[4]
         pu_1 = 0.25 * y1 * across_dense(x2_1, scr[0], dlane)
-        pv_2 = (0.25 * sigma) * got(ref, 2, "h") * (x2_3 - x2_1)
-        kept.append((senses[0] + across_dense(pu_1, scr[1], dlane) + sigma * pv_2, x2_2, y1, w0_1))
-    for c in blocks:
-        at = cut(c)
-        wet = wet_ref[cut(c, total), :].astype(jnp.float32)
+        pv_2 = (0.25 * sigma) * h2 * (x2_3 - x2_1)
+        kept.append((senses[0] + across_dense(pu_1, scr[1], dlane) + sigma * pv_2, x2_2, y1, got["w0"]))
+    for c in blocks:
+        at = cut(c)
         b2 = (1.0 + ms[at, :]) * s2_ref[at, :] - sv_ref[at, :] - vs[at, :]
         b2s[at, :] = b2
-        x2p[cut(c, ROWS), :] = wet * b2
-    for (ref, sigma, edge, scr), (part, x2_2, y1, w0_1) in zip(sides, kept):
+        x2p[cut(c, ROWS), :] = wet_ref[cut(c, total), :].astype(jnp.float32) * b2
+    arrive(5, 6, 7, 8, 9, 10, 11, 12)
+    for (sigma, edge, scr), (part, x2_2, y1, w0_1) in zip(sides, kept):
         pvr[pl.ds(edge, tiles, stride=ROWS), :] = (0.25 * sigma) * y1 * (x2_2 - row_of(x2p, edge, tiles, ROWS))
     for c in blocks:
         at = cut(c)
@@ -334,13 +357,13 @@
         au1[at, :] = y * a_u2 - pull * u1_ref[at, :]
         av1[at, :] = y * a_v2 - pull * v1_ref[at, :]
         vs[at, :] = energy * t2_ref[at, :]
-    for (ref, sigma, edge, scr), (part, x2_2, y1, w0_1) in zip(sides, kept):
+    for (sigma, edge, scr), (part, x2_2, y1, w0_1) in zip(sides, kept):
         x1r[pl.ds(edge, tiles, stride=ROWS), :] = w0_1 * (part - sigma * row_of(pvp, edge, tiles, ROWS))
     for c in blocks:
         at = cut(c)
-        wet = wet_ref[at, :].astype(jnp.float32)
         a_s1 = b2s[at, :] + across(pup, c, STEP, lane) + along(pvp, pvr, c, STEP, sub)
-        x1p[cut(c, ROWS), :] = wet * a_s1
+        x1p[cut(c, ROWS), :] = wet_ref[at, :].astype(jnp.float32) * a_s1
+    arrive(13)
     for c in blocks:
         at = cut(c)
         a_u1 = au1[at, :] + 0.25 * across(x1p, c, STEP, lane)
@@ -349,7 +372,7 @@
         grad_ref[at, :] = -(energy * t0_ref[at, :] + vs[at, :])
 
 
-def gauge_kernel(tile_ref, cell_ref, value_ref, out_ref):
+def gauge_table(tile_ref, cell_ref, value_ref, out_ref):
     strips = out_ref.shape[0]
     listed = tile_ref.shape[1]
     hit = lax.broadcasted_iota(jnp.int32, (strips, listed), 0) == tile_ref[...]
@@ -384,15 +407,54 @@
         out_ref[:, LANES * k : LANES * (k + 1)] = acc
 
 
-def call(kernel, outs, scratch, name):
-    shapes = [jax.ShapeDtypeStruct(o, jnp.float32) for o in outs]
+def call(body, ins, outs, scratch, name):
+    count, given = len(ins), len(outs)
+    moved = [i for i, (_, lead) in enumerate(ins) if lead is not HERE]
+    copied = [i for i, (shape, kept) in enumerate(outs) if not kept]
+
+    def kernel(*refs):
+        sources, results, rest = refs[:count], refs[count : count + given], refs[count + given :]
+        landed, left, own = rest[: len(moved)], rest[len(moved) : len(moved) + len(copied)], rest[len(moved) + len(copied) : -2]
+        into, out_of = rest[-2:]
+        operands, arrivals = list(sources), {}
+        for j, i in enumerate(moved):
+            lead, target = ins[i][1], landed[j]
+            operands[i] = target
+            if lead:
+                target = target.at[pl.ds(lead, sources[i].shape[0])]
+            arrivals[i] = pltpu.make_async_copy(sources[i], target, into.at[j])
+            arrivals[i].start()
+        places, departures = list(results), {}
+        for j, i in enumerate(copied):
+            departures[i] = pltpu.make_async_copy(left[j], results[i], out_of.at[j])
+            places[i] = left[j]
+
+        def arrive(*which):
+            for i in which:
+                arrivals[i].wait()
+
+        def leave(*which):
+            for i in which:
+                departures[i].start()
+
+        body(*operands, *places, *own, arrive=arrive, leave=leave)
+        for departure in departures.values():
+            departure.wait()
+
     return pl.pallas_call(
         kernel,
-        out_shape=shapes if len(shapes) > 1 else shapes[0],
-        scratch_shapes=[pltpu.VMEM(s, jnp.float32) for s in scratch],
+        out_shape=[(jax.ShapeDtypeStruct if kept else pltpu.HBM)(shape, jnp.float32) for shape, kept in outs],
+        in_specs=[pl.BlockSpec(memory_space=pltpu.VMEM if lead is HERE else pltpu.HBM) for _, lead in ins],
+        out_specs=[pl.BlockSpec(memory_space=pltpu.VMEM if kept else pltpu.HBM) for _, kept in outs],
+        scratch_shapes=[
+            pltpu.VMEM((ins[i][0].shape[0] + 2 * ins[i][1], ins[i][0].shape[1]), ins[i][0].dtype) for i in moved
+        ]
+        + [pltpu.VMEM(outs[i][0], jnp.float32) for i in copied]
+        + [pltpu.VMEM(shape, jnp.float32) for shape in scratch]
+        + [pltpu.SemaphoreType.DMA((len(moved),)), pltpu.SemaphoreType.DMA((max(1, len(copied)),))],
         name=name,
-        compiler_params=pltpu.CompilerParams(vmem_limit_bytes=48 * 1024 * 1024),
-    )
+        compiler_params=pltpu.CompilerParams(vmem_limit_bytes=GRANT),
+    )(*(x if lead is HERE else pltpu.with_memory_space_constraint(x, pltpu.HBM) for x, lead in ins))
 
 
 def tiled(field):
@@ -418,28 +480,39 @@
     s0, u0, v0, depth, rough, wet, survey = (tiled(f) for f in (s0[0], u0[0], v0[0], depth, rough, wet[0], survey[0]))
     field, padded, dense = (total, LANES), (total + 2 * ROWS, LANES), (tiles + 2 * ROWS, LANES)
     packet = (len(SENT) * tiles, LANES)
-    down, up, u1, v1i, b, q1, k, t0, kr = call(
-        prepare_kernel, [packet, packet] + [field] * 7, [padded] * 6 + [field] * 4, "prepare"
-    )(s0, u0, v0, depth, rough, wet, survey)
+    listed = (1, gauge_cells.shape[1])
+    lists = [(x.reshape(listed), 0) for x in (gauge_tiles, gauge_cells, gauge_values)]
+    down, up, send, edges, u1, v1i, q1, k, t0, kr = call(
+        prepare_kernel,
+        lists + [(s0, ROWS)] + [(x, 0) for x in (depth, rough, u0, v0, wet, survey)],
+        [(packet, True), (packet, True), ((strips, LANES), True), ((2 * len(EDGES) * tiles, LANES), False)]
+        + [(field, False)] * 6,
+        [padded] * 5 + [field] * 6,
+        "prepare",
+    )
     from_above = shifted(down, "tile", 1)
     from_below = shifted(up, "tile", -1)
-    listed = gauge_cells.shape[1]
-    send = call(gauge_kernel, [(strips, LANES)], [], "gauges")(
-        gauge_tiles.reshape(1, listed), gauge_cells.reshape(1, listed), gauge_values.reshape(1, listed)
-    )
     gauges = lax.all_to_all(send, "tile", 0, 0, tiled=True)
-    rim_pass = (2 * len(PASS) * tiles, LANES)
     v1, s2, u2, v2, y, yh, t2, kk, passed = call(
-        forward_kernel, [field] * 8 + [rim_pass], [padded] * 4 + [field] * 3 + [dense] * 6, "forward"
-    )(from_above, from_below, s0, depth, wet, u1, v1i, b, q1, k, kr)
-    grad = call(
-        backward_kernel, [field],
+        forward_kernel,
+        [(edges, 0), (from_above, HERE), (from_below, HERE)] + [(x, 0) for x in (v1i, q1, wet, u1, k, depth, kr)],
+        [(field, False)] * 8 + [((2 * len(PASS) * tiles, LANES), False)],
+        [padded] * 4 + [field] * 3 + [dense] * 6,
+        "forward",
+    )
+    (grad,) = call(
+        backward_kernel,
+        [(gauges, HERE)] + [(x, 0) for x in (s2, survey, wet, passed, u2, v2, kk, y, yh, u1, v1, t2, t0)],
+        [(field, True)],
         [padded, field, padded, padded, field, padded, field, field, field, field, field, field]
         + [(6 * tiles, LANES)] * 2 + [dense] * 4,
         "backward",
-    )(gauges, from_above, from_below, passed, wet, survey, u1, v1, s2, u2, v2, y, yh, t2, kk, t0)
+    )
     parts = lax.all_to_all(grad.reshape(events, total // events, LANES), "event", 0, 0, tiled=True)
-    return call(sum_kernel, [(ROWS, col_count // events)], [], "total")(parts)
+    return pl.pallas_call(
+        sum_kernel, out_shape=jax.ShapeDtypeStruct((ROWS, col_count // events), jnp.float32), name="total",
+        compiler_params=pltpu.CompilerParams(vmem_limit_bytes=GRANT),
+    )(parts)
 
 
 def solution(mesh):

time: 76.5 us -> 59.9 us (0.78)
  local copies, waits for them, and re-layouts: 28.2 us -> 0 us
  waiting for transfers between devices: 1.93 us -> 9.53 us
  Pallas kernels: 6.22 us -> 11.1 us
    unnamed x80 -> x0, local copies, waits for them, and re-layouts: 28.2 us -> none
    all_to_all x1, waiting for transfers between devices: 1.92 us -> 9.53 us  [per_device(): gauges = lax.all_to_all(send, 'tile', 0, 0, tiled=True)]
    pallas_call x5 -> x4, Pallas kernels: 6.22 us -> 11.1 us  [the longest x3 10.4 us: call(): pl.pallas_call(kernel, out_shape=[(jax.ShapeDtypeStruct if kept else pltp...]
  transfers between devices with their start and end apart: 3 -> 3, of which waited for: 1 -> 1; matrix products, arithmetic and copies ran while one was open for 0% -> 0% of each run, Pallas kernels for 3% -> 6%
where the time goes in v2:
time: 59.9 us; the launch traced here: 59.6 us
  starting transfers between devices  25.6 us (43%)
  blocking collectives  13.3 us (22%)
  Pallas kernels  11.1 us (19%)
  waiting for transfers between devices  9.53 us (16%)
    all_to_all x1, starting transfers between devices, per_device(): gauges = lax.all_to_all(send, 'tile', 0, 0, tiled=True)  19.9 us
    all_to_all x1, blocking collectives, per_device(): lax.all_to_all(grad.reshape(events, total // events, LANES), 'event', 0,...  13.3 us
    pallas_call x3, Pallas kernels, call(): pl.pallas_call(kernel, out_shape=[(jax.ShapeDtypeStruct if kept else pltp...  10.4 us
    all_to_all x1, waiting for transfers between devices, per_device(): gauges = lax.all_to_all(send, 'tile', 0, 0, tiled=True)  9.53 us
    ppermute x2, starting transfers between devices, shifted(): lax.ppermute(value, axis, [(i, i + steps) for i in range(initial, last)])  5.69 us
  transfers between devices with their start and end apart: 3, of which 1 were waited for; matrix products, arithmetic and copies ran while one was open for 0% of the time, Pallas kernels for 6%

profile of v2, /device:TPU:1, one launch (start us, length us, event | category | flops | bytes accessed | tf_op | source)
XLA Modules:
  0.0 59.6 jit_solution(6755585294269539340)
XLA Ops:
  0.0 3.9 %prepare.1 = (f32[1152,128]{1,0:T(8,128)S(1)}, f32[1152,128]{1,0:T(8,128)S(1)}, f32[64,128]{1,0:T(8,128)}, f32[384,128]{1,0:T(8,128)}, f32[512,128]{1,0:T(8,128)...) custom-call(s32[1,256]{1,0:T(1,128)} %bitcast.54, ...), custom_call_target="tpu_custom_call" | custom-call | tf_op jit(solution)/shard_map/prepare/pallas_call | solution.py:444
  3.9 4.4 %collective-permute-start = (f32[1152,128]{1,0:T(8,128)S(1)}, f32[1152,128]{1,0:T(8,128)S(1)}, u32[]{:S(2)}, u32[]{:S(2)}) collective-permute-start(f32[1152,128]{1,0:T(8,128)S(1)} %get-tuple-element.26), channel_id=1, source_target_pairs={{0,1},{1,2},{2,3},{3,4},{4,5},{5,6},{6,7},{7,8},{8,9},{9,10},{10,1... | collective-permute-start | bytes 1769480 | tf_op jit(solution)/shard_map/ppermute | solution.py:470
  8.3 1.3 %collective-permute-start.1 = (f32[1152,128]{1,0:T(8,128)S(1)}, f32[1152,128]{1,0:T(8,128)S(1)}, u32[]{:S(2)}, u32[]{:S(2)}) collective-permute-start(f32[1152,128]{1,0:T(8,128)S(1)} %get-tuple-element.27), channel_id=1, source_target_pairs={{1,0},{2,1},{3,2},{4,3},{5,4},{6,5},{7,6},{8,7},{9,8},{10,9},{11,1... | collective-permute-start | bytes 1769480 | tf_op jit(solution)/shard_map/ppermute | solution.py:470
  9.6 19.9 %all-to-all-start = ((f32[64,1,128]{2,1,0:T(1,128)}), f32[64,1,128]{2,1,0:T(1,128)S(1)}, u32[]{:S(2)}, u32[]{:S(2)}) async-start(f32[64,1,128]{2,1,0:T(1,128)} %bitcast.23), calls=%async_computation | async-start | bytes 65536 | tf_op jit(solution)/shard_map/all_to_all | solution.py:495
  29.5 0.0 collective-permute-done.refs_1_
  29.6 0.0 collective-permute-done.1.refs_2_
  29.6 3.7 %forward.1 = (f32[512,128]{1,0:T(8,128)}, f32[512,128]{1,0:T(8,128)}, f32[512,128]{1,0:T(8,128)}, f32[512,128]{1,0:T(8,128)}, f32[512,128]{1,0:T(8,128)}, /*inde...) custom-call(f32[384,128]{1,0:T(8,128)} %get-tuple-element.25.refs_0_, ...), custom_call_target="tpu_custom_call" | custom-call | tf_op jit(solution)/shard_map/forward/pallas_call | solution.py:444
  33.3 9.5 %all-to-all-done = f32[64,1,128]{2,1,0:T(1,128)S(1)} async-done(((f32[64,1,128]{2,1,0:T(1,128)}), f32[64,1,128]{2,1,0:T(1,128)S(1)}, u32[]{:S(2)}, u32[]{:S(2)}) %all-to-all-start) | async-done | bytes 32800 | tf_op jit(solution)/shard_map/all_to_all | solution.py:495
  42.8 2.8 %backward.1 = f32[512,128]{1,0:T(8,128)S(1)} custom-call(f32[64,128]{1,0:T(8,128)S(1)} %bitcast.42, f32[512,128]{1,0:T(8,128)} %get-tuple-element.33.refs_1_, f32[512,128]{1,0:T(8,128)} %bitcast.47, s32[1024,128]{1,0:T(8,128)} %bitcast.45, f32[1280,128]{1,0:T(8,128)} %get-tuple-element.34.refs_4_, f32[512,128]{1,0:T(8,128)} %get-tuple-element.35.refs_5_, ...), custom_call_target="tpu_custom_call" | custom-call | tf_op jit(solution)/shard_map/backward/pallas_call | solution.py:444
  45.6 13.3 %all_to_all.16.x_ref = f32[8,64,128]{2,1,0:T(8,128)S(1)} all-to-all(f32[8,64,128]{2,1,0:T(8,128)S(1)} %bitcast.41), channel_id=1, replica_groups=mesh['event'=8,'tile'=64] {'event'}, dimensions={0} | all-to-all | bytes 524288 | tf_op jit(solution)/shard_map/all_to_all | solution.py:511
  59.0 0.6 %total.1 = f32[8,1024]{1,0:T(8,128)} custom-call(f32[8,64,128]{2,1,0:T(8,128)S(1)} %all_to_all.16.x_ref), custom_call_target="tpu_custom_call" | custom-call | tf_op jit(solution)/shard_map/total/pallas_call | solution.py:512
Async XLA Ops:
  3.9 25.6 %collective-permute-start = (f32[1152,128]{1,0:T(8,128)S(1)}, f32[1152,128]{1,0:T(8,128)S(1)}, u32[]{:S(2)}, u32[]{:S(2)}) collective-permute-start(f32[1152,128]{1,0:T(8,128)S(1)} %get-tuple-element.26), channel_id=1, source_target_pairs={{0,1},{1,2},{2,3},{3,4},{4,5},{5,6},{6,7},{7,8},{8,9},{9,10},{10,1... | collective-permute-start | bytes 1769480 | tf_op jit(solution)/shard_map/ppermute | solution.py:470
  8.3 21.2 %collective-permute-start.1 = (f32[1152,128]{1,0:T(8,128)S(1)}, f32[1152,128]{1,0:T(8,128)S(1)}, u32[]{:S(2)}, u32[]{:S(2)}) collective-permute-start(f32[1152,128]{1,0:T(8,128)S(1)} %get-tuple-element.27), channel_id=1, source_target_pairs={{1,0},{2,1},{3,2},{4,3},{5,4},{6,5},{7,6},{8,7},{9,8},{10,9},{11,1... | collective-permute-start | bytes 1769480 | tf_op jit(solution)/shard_map/ppermute | solution.py:470
  9.6 33.2 %all-to-all-start = ((f32[64,1,128]{2,1,0:T(1,128)}), f32[64,1,128]{2,1,0:T(1,128)S(1)}, u32[]{:S(2)}, u32[]{:S(2)}) async-start(f32[64,1,128]{2,1,0:T(1,128)} %bitcast.23), calls=%async_computation | async-start | bytes 65536 | tf_op jit(solution)/shard_map/all_to_all | solution.py:495

commit v3 on v2

--- a/solution.py
+++ b/solution.py
@@ -11,6 +11,8 @@
 STEP = 4
 GRANT = 16 * 1024 * 1024
 HERE = None
+STRIP_LEAD = 42
+EVENT_LEAD = 4
 RIM1 = ("s0", "v1", "b", "s1", "r", "u1", "k", "sv")
 RIM2 = ("s1", "w0", "v2", "h", "u2", "sv")
 RIM3 = ("v2", "h", "s2", "sv")
@@ -276,7 +278,7 @@
 def backward_kernel(
     gauge_ref, s2_ref, sv_ref, wet_ref, pass_ref, u2_ref, v2_ref, kk_ref, y_ref, yh_ref, u1_ref, v1_ref, t2_ref, t0_ref,
     grad_ref,
-    x2p, x2r, pup, pvp, pvr, x1p, x1r, b2s, au1, av1, vs, ms, vt, mt, da, db, dc, dd, *, arrive, leave,
+    x2p, x2r, pup, pvp, pvr, x1p, x1r, b2s, au1, av1, vs, ms, vt, mt, da, db, dc, dd, *, arrive, leave, shift,
 ):
     total = s2_ref.shape[0]
     tiles = total // ROWS
@@ -369,13 +371,18 @@
         a_u1 = au1[at, :] + 0.25 * across(x1p, c, STEP, lane)
         a_v1 = av1[at, :] + 0.25 * along(x1p, x1r, c, STEP, sub)
         energy = a_u1 * u1_ref[at, :] + a_v1 * v1_ref[at, :]
-        grad_ref[at, :] = -(energy * t0_ref[at, :] + vs[at, :])
+        grad_ref[cut((c - shift) % tiles), :] = -(energy * t0_ref[at, :] + vs[at, :])
+
+
+def turned_order(count, first):
+    return [(i + first) % count for i in range(count)]
 
 
 def gauge_table(tile_ref, cell_ref, value_ref, out_ref):
     strips = out_ref.shape[0]
     listed = tile_ref.shape[1]
-    hit = lax.broadcasted_iota(jnp.int32, (strips, listed), 0) == tile_ref[...]
+    first = STRIP_LEAD * strips // 64
+    hit = (lax.broadcasted_iota(jnp.int32, (strips, listed), 0) + first) % strips == tile_ref[...]
     earlier = lax.broadcasted_iota(jnp.int32, (listed, listed), 0) < lax.broadcasted_iota(jnp.int32, (listed, listed), 1)
     rank = jnp.dot(
         jnp.where(hit, 1.0, 0.0).astype(jnp.bfloat16), jnp.where(earlier, 1.0, 0.0).astype(jnp.bfloat16),
@@ -385,7 +392,7 @@
     cell = cell_ref[...].astype(jnp.float32) + 1.0
     value = value_ref[...]
     lane = lax.broadcasted_iota(jnp.int32, (strips, LANES), 1)
-    line = lax.broadcasted_iota(jnp.int32, (strips, LANES), 0)
+    line = (lax.broadcasted_iota(jnp.int32, (strips, LANES), 0) + first) % strips
     own = jnp.full((strips, LANES), -1.0, jnp.float32)
     for k in range(8):
         taken = rank == float(k)
@@ -492,7 +499,7 @@
     )
     from_above = shifted(down, "tile", 1)
     from_below = shifted(up, "tile", -1)
-    gauges = lax.all_to_all(send, "tile", 0, 0, tiled=True)
+    gauges = lax.all_to_all(send, "tile", 0, 0, axis_index_groups=[turned_order(strips, STRIP_LEAD * strips // 64)], tiled=True)
     v1, s2, u2, v2, y, yh, t2, kk, passed = call(
         forward_kernel,
         [(edges, 0), (from_above, HERE), (from_below, HERE)] + [(x, 0) for x in (v1i, q1, wet, u1, k, depth, kr)],
@@ -500,15 +507,16 @@
         [padded] * 4 + [field] * 3 + [dense] * 6,
         "forward",
     )
+    order = turned_order(events, EVENT_LEAD * events // 8)
     (grad,) = call(
-        backward_kernel,
+        functools.partial(backward_kernel, shift=order[0] * (tiles // events)),
         [(gauges, HERE)] + [(x, 0) for x in (s2, survey, wet, passed, u2, v2, kk, y, yh, u1, v1, t2, t0)],
         [(field, True)],
         [padded, field, padded, padded, field, padded, field, field, field, field, field, field]
         + [(6 * tiles, LANES)] * 2 + [dense] * 4,
         "backward",
     )
-    parts = lax.all_to_all(grad.reshape(events, total // events, LANES), "event", 0, 0, tiled=True)
+    parts = lax.all_to_all(grad.reshape(events, total // events, LANES), "event", 0, 0, axis_index_groups=[order], tiled=True)
     return pl.pallas_call(
         sum_kernel, out_shape=jax.ShapeDtypeStruct((ROWS, col_count // events), jnp.float32), name="total",
         compiler_params=pltpu.CompilerParams(vmem_limit_bytes=GRANT),

time: 59.9 us -> 53.5 us (0.89)
  the two profiles are of different devices: /device:TPU:1 before, /device:TPU:33 now
where the time goes in v3:
time: 53.5 us; the launch traced here: 53.2 us
  starting transfers between devices  26.2 us (49%)
  blocking collectives  12.1 us (23%)
  Pallas kernels  11.1 us (21%)
  waiting for transfers between devices  3.82 us (7%)
    all_to_all x1, starting transfers between devices, per_device(): lax.all_to_all(send, 'tile', 0, 0, axis_index_groups=[turned_order(strips...  20.7 us
    all_to_all x1, blocking collectives, per_device(): lax.all_to_all(grad.reshape(events, total // events, LANES), 'event', 0,...  12.1 us
    pallas_call x3, Pallas kernels, call(): pl.pallas_call(kernel, out_shape=[(jax.ShapeDtypeStruct if kept else pltp...  10.4 us
    ppermute x2, starting transfers between devices, shifted(): lax.ppermute(value, axis, [(i, i + steps) for i in range(initial, last)])  5.47 us
    all_to_all x1, waiting for transfers between devices, per_device(): lax.all_to_all(send, 'tile', 0, 0, axis_index_groups=[turned_order(strips...  3.81 us
  transfers between devices with their start and end apart: 3, of which 1 were waited for; matrix products, arithmetic and copies ran while one was open for 0% of the time, Pallas kernels for 7%

profile of v3, /device:TPU:33, one launch (start us, length us, event | category | flops | bytes accessed | tf_op | source)
XLA Modules:
  0.0 53.2 jit_solution(15715580815765136207)
XLA Ops:
  0.0 3.9 %prepare.1 = (f32[1152,128]{1,0:T(8,128)S(1)}, f32[1152,128]{1,0:T(8,128)S(1)}, f32[64,128]{1,0:T(8,128)}, f32[384,128]{1,0:T(8,128)}, f32[512,128]{1,0:T(8,128)...) custom-call(s32[1,256]{1,0:T(1,128)} %bitcast.54, ...), custom_call_target="tpu_custom_call" | custom-call | tf_op jit(solution)/shard_map/prepare/pallas_call | solution.py:451
  3.9 3.5 %collective-permute-start = (f32[1152,128]{1,0:T(8,128)S(1)}, f32[1152,128]{1,0:T(8,128)S(1)}, u32[]{:S(2)}, u32[]{:S(2)}) collective-permute-start(f32[1152,128]{1,0:T(8,128)S(1)} %get-tuple-element.26), channel_id=1, source_target_pairs={{0,1},{1,2},{2,3},{3,4},{4,5},{5,6},{6,7},{7,8},{8,9},{9,10},{10,1... | collective-permute-start | bytes 1769480 | tf_op jit(solution)/shard_map/ppermute | solution.py:477
  7.5 1.9 %collective-permute-start.1 = (f32[1152,128]{1,0:T(8,128)S(1)}, f32[1152,128]{1,0:T(8,128)S(1)}, u32[]{:S(2)}, u32[]{:S(2)}) collective-permute-start(f32[1152,128]{1,0:T(8,128)S(1)} %get-tuple-element.27), channel_id=1, source_target_pairs={{1,0},{2,1},{3,2},{4,3},{5,4},{6,5},{7,6},{8,7},{9,8},{10,9},{11,1... | collective-permute-start | bytes 1769480 | tf_op jit(solution)/shard_map/ppermute | solution.py:477
  9.4 20.7 %all-to-all-start = ((f32[64,1,128]{2,1,0:T(1,128)}), f32[64,1,128]{2,1,0:T(1,128)S(1)}, u32[]{:S(2)}, u32[]{:S(2)}) async-start(f32[64,1,128]{2,1,0:T(1,128)} %bitcast.23), calls=%async_computation | async-start | bytes 65536 | tf_op jit(solution)/shard_map/all_to_all | solution.py:502
  30.2 0.0 collective-permute-done.refs_1_
  30.2 0.0 collective-permute-done.1.refs_2_
  30.2 3.7 %forward.1 = (f32[512,128]{1,0:T(8,128)}, f32[512,128]{1,0:T(8,128)}, f32[512,128]{1,0:T(8,128)}, f32[512,128]{1,0:T(8,128)}, f32[512,128]{1,0:T(8,128)}, /*inde...) custom-call(f32[384,128]{1,0:T(8,128)} %get-tuple-element.25.refs_0_, ...), custom_call_target="tpu_custom_call" | custom-call | tf_op jit(solution)/shard_map/forward/pallas_call | solution.py:451
  33.9 3.8 %all-to-all-done = f32[64,1,128]{2,1,0:T(1,128)S(1)} async-done(((f32[64,1,128]{2,1,0:T(1,128)}), f32[64,1,128]{2,1,0:T(1,128)S(1)}, u32[]{:S(2)}, u32[]{:S(2)}) %all-to-all-start) | async-done | bytes 32800 | tf_op jit(solution)/shard_map/all_to_all | solution.py:502
  37.7 2.8 %backward.1 = f32[512,128]{1,0:T(8,128)S(1)} custom-call(f32[64,128]{1,0:T(8,128)S(1)} %bitcast.42, f32[512,128]{1,0:T(8,128)} %get-tuple-element.33.refs_1_, f32[512,128]{1,0:T(8,128)} %bitcast.47, s32[1024,128]{1,0:T(8,128)} %bitcast.45, f32[1280,128]{1,0:T(8,128)} %get-tuple-element.34.refs_4_, f32[512,128]{1,0:T(8,128)} %get-tuple-element.35.refs_5_, ...), custom_call_target="tpu_custom_call" | custom-call | tf_op jit(solution)/shard_map/backward/pallas_call | solution.py:451
  40.5 12.1 %all_to_all.16.x_ref = f32[8,64,128]{2,1,0:T(8,128)S(1)} all-to-all(f32[8,64,128]{2,1,0:T(8,128)S(1)} %bitcast.41), channel_id=1, replica_groups={{256,320,384,448,0,64,128,192},{257,321,385,449,1,65,129,193},{258,322,..., dimensions={0} | all-to-all | bytes 524288 | tf_op jit(solution)/shard_map/all_to_all | solution.py:519
  52.6 0.6 %total.1 = f32[8,1024]{1,0:T(8,128)} custom-call(f32[8,64,128]{2,1,0:T(8,128)S(1)} %all_to_all.16.x_ref), custom_call_target="tpu_custom_call" | custom-call | tf_op jit(solution)/shard_map/total/pallas_call | solution.py:520
Async XLA Ops:
  3.9 26.2 %collective-permute-start = (f32[1152,128]{1,0:T(8,128)S(1)}, f32[1152,128]{1,0:T(8,128)S(1)}, u32[]{:S(2)}, u32[]{:S(2)}) collective-permute-start(f32[1152,128]{1,0:T(8,128)S(1)} %get-tuple-element.26), channel_id=1, source_target_pairs={{0,1},{1,2},{2,3},{3,4},{4,5},{5,6},{6,7},{7,8},{8,9},{9,10},{10,1... | collective-permute-start | bytes 1769480 | tf_op jit(solution)/shard_map/ppermute | solution.py:477
  7.5 22.7 %collective-permute-start.1 = (f32[1152,128]{1,0:T(8,128)S(1)}, f32[1152,128]{1,0:T(8,128)S(1)}, u32[]{:S(2)}, u32[]{:S(2)}) collective-permute-start(f32[1152,128]{1,0:T(8,128)S(1)} %get-tuple-element.27), channel_id=1, source_target_pairs={{1,0},{2,1},{3,2},{4,3},{5,4},{6,5},{7,6},{8,7},{9,8},{10,9},{11,1... | collective-permute-start | bytes 1769480 | tf_op jit(solution)/shard_map/ppermute | solution.py:477
  9.4 28.3 %all-to-all-start = ((f32[64,1,128]{2,1,0:T(1,128)}), f32[64,1,128]{2,1,0:T(1,128)S(1)}, u32[]{:S(2)}, u32[]{:S(2)}) async-start(f32[64,1,128]{2,1,0:T(1,128)} %bitcast.23), calls=%async_computation | async-start | bytes 65536 | tf_op jit(solution)/shard_map/all_to_all | solution.py:502

commit v4 on v3

--- a/solution.py
+++ b/solution.py
@@ -12,14 +12,15 @@
 GRANT = 16 * 1024 * 1024
 HERE = None
 STRIP_LEAD = 42
+STRIP_STRIDE = 1
 EVENT_LEAD = 4
 RIM1 = ("s0", "v1", "b", "s1", "r", "u1", "k", "sv")
-RIM2 = ("s1", "w0", "v2", "h", "u2", "sv")
-RIM3 = ("v2", "h", "s2", "sv")
+RIM2 = ("s1", "w0", "v2", "h", "s2", "sv")
+RIM3 = ("h", "s2", "sv")
 SENT = tuple((1, x) for x in RIM1) + tuple((2, x) for x in RIM2) + tuple((3, x) for x in RIM3)
 SLOT = {key: i for i, key in enumerate(SENT)}
 PASS = ("s2_1", "s2_2", "s2_3", "y1", "w0", "h2", "h3", "sv1", "sv2", "sv3")
-EDGES = ((1, "s0"), (1, "v1"), (1, "b"))
+EDGES = 3
 
 
 def masks(rows):
@@ -76,6 +77,7 @@
     clear_ends(s0p, u1p, v1p, s1p, u2p, v2p)
     arrive(0, 1, 2)
     gauge_table(tile_ref, cell_ref, value_ref, send_ref)
+    leave(2)
     arrive(3, 4, 5, 6, 7, 8)
     blocks = range(0, tiles, STEP)
 
@@ -88,7 +90,8 @@
         wet = wet_ref[at, :].astype(jnp.float32)
         kr = 4.0 * rough * jnp.exp((-4.0 / 3.0) * jnp.log(depth))
         k = 0.5 * kr * rough
-        speed = jnp.sqrt(east * east + north * north + 1.0)
+        square = east * east + north * north + 1.0
+        speed = square * lax.rsqrt(square)
         inverse = 1.0 / (1.0 + k * speed)
         y = wet * inverse
         b = 0.2 * depth * y
@@ -103,7 +106,11 @@
         kr_ref[at, :] = kr
         t0_ref[at, :] = kr * speed * inverse
         w0q[at, :] = 0.25 * wet
-    leave(4, 5, 7, 8, 9)
+    for i, (ref, lead) in enumerate(((s0p, ROWS), (v1_ref, 0), (b_ref, 0))):
+        for j, row in enumerate((0, ROWS - 1)):
+            first = (j * EDGES + i) * tiles
+            edge_ref[first : first + tiles, :] = row_of(ref, row, tiles, lead)
+    leave(3, 4, 5, 7, 8, 9)
     for c in blocks:
         at = cut(c)
         quarter = w0q[at, :]
@@ -116,13 +123,15 @@
         wet = wet_ref[cut(c, total), :].astype(jnp.float32)
         east, north = u1_ref[at, :], v1_ref[at, :]
         depth = 0.2 * h_ref[at, :]
-        y = wet / (1.0 + k_ref[at, :] * jnp.sqrt(east * east + north * north + 1.0))
+        square = east * east + north * north + 1.0
+        y = wet / (1.0 + k_ref[at, :] * (square * lax.rsqrt(square)))
         h = depth * y
         hh[at, :] = h
         rr[at, :] = depth * wet
         w1_ref[at, :] = wet
         u2p[cut(c, ROWS), :] = y * east - h * across(s1p, c, STEP, lane)
-        v2p[cut(c, ROWS), :] = y * north - h * along(s1p, None, c, STEP, sub)
+        v2 = y * north - h * along(s1p, None, c, STEP, sub)
+        v2p[cut(c, ROWS), :] = jnp.where((sub == 0) | (sub == ROWS - 1), 0.0, v2)
     for c in blocks:
         at = cut(c)
         change = across(u2p, c, STEP, lane) + along(v2p, None, c, STEP, sub)
@@ -131,16 +140,9 @@
         (1, "s0"): (s0p, ROWS), (1, "v1"): (v1_ref, 0), (1, "b"): (b_ref, 0), (1, "s1"): (s1p, ROWS),
         (1, "r"): (rr, 0), (1, "u1"): (u1_ref, 0), (1, "k"): (k_ref, 0), (1, "sv"): (sv_ref, 0),
         (2, "s1"): (s1p, ROWS), (2, "w0"): (w0q, 0), (2, "v2"): (v2p, ROWS), (2, "h"): (hh, 0),
-        (2, "u2"): (u2p, ROWS), (2, "sv"): (sv_ref, 0),
-        (3, "v2"): (v2p, ROWS), (3, "h"): (hh, 0), (3, "s2"): (s2p, 0), (3, "sv"): (sv_ref, 0),
+        (2, "s2"): (s2p, 0), (2, "sv"): (sv_ref, 0), (3, "h"): (hh, 0), (3, "s2"): (s2p, 0), (3, "sv"): (sv_ref, 0),
     }
     arrive(9)
-    for i, key in enumerate(EDGES):
-        ref, lead = held[key]
-        for j, row in enumerate((0, ROWS - 1)):
-            first = (j * len(EDGES) + i) * tiles
-            edge_ref[first : first + tiles, :] = row_of(ref, row, tiles, lead)
-    leave(3)
     for key, place in SLOT.items():
         ref, lead = held[key]
         down_ref[place * tiles : (place + 1) * tiles, :] = row_of(ref, ROWS - key[0], tiles, lead)
@@ -169,7 +171,7 @@
         return ref[place * tiles : (place + 1) * tiles, :]
 
     def own(edge, i):
-        first = (len(EDGES) * (edge > 0) + i) * tiles
+        first = (EDGES * (edge > 0) + i) * tiles
         return edge_ref[first : first + tiles, :]
 
     arrive(0, 3)
@@ -192,11 +194,11 @@
         inverse = 1.0 / (1.0 + got(ref, 1, "k") * jnp.sqrt(u1_1 * u1_1 + v1_1 * v1_1 + 1.0))
         v2i_2 = got(ref, 2, "v2")
         v2_2 = v2i_2 + 0.25 * w0_1 * h2 * v1_e
-        v2_3 = got(ref, 3, "v2") + sigma * h3 * bump
-        u2_2 = got(ref, 2, "u2") - h2 * across_dense(bump, scr[0], dlane)
+        v2_3 = sigma * h3 * bump
+        u2_2 = -h2 * across_dense(bump, scr[0], dlane)
         s2_3 = got(ref, 3, "s2") + (0.25 * sigma) * jnp.where(h3 > 0.0, 1.0, 0.0) * (v2_2 - v2i_2)
         u2_1 = (w1_1 * u1_1 - r * across_dense(s1_1, scr[1], dlane)) * inverse
-        kept.append((v1_1, s1_1, s1_2, w0_1, w1_1, r, inverse, h2, v2_2, v2_3, u2_1, u2_2, s2_3))
+        kept.append((v1_1, s1_1, s1_2, w0_1, w1_1, r, inverse, h2, v2_2, v2_3, u2_1, u2_2, s2_3, bump))
     arrive(4, 5)
     for c in blocks:
         at = cut(c)
@@ -207,12 +209,12 @@
     arrive(6, 7, 8, 9)
     late = []
     for (ref, sigma, edge, scr), values in zip(sides, kept):
-        v1_1, s1_1, s1_2, w0_1, w1_1, r, inverse, h2, v2_2, v2_3, u2_1, u2_2, s2_3 = values
+        v1_1, s1_1, s1_2, w0_1, w1_1, r, inverse, h2, v2_2, v2_3, u2_1, u2_2, s2_3, bump = values
         s1_e = row_of(s1p, edge, tiles, ROWS)
         v2_1 = (w1_1 * v1_1 - sigma * r * (s1_2 - s1_e)) * inverse
         v2r[pl.ds(edge, tiles, stride=ROWS), :] = v2_1
         w1_2 = jnp.where(h2 > 0.0, 0.25, 0.0)
-        s2_2 = s1_2 - w1_2 * (across_dense(u2_2, scr[2], dlane) + sigma * (v2_3 - v2_1))
+        s2_2 = got(ref, 2, "s2") + bump - w1_2 * (across_dense(u2_2, scr[2], dlane) + sigma * (v2_3 - v2_1))
         late.append((s2_2, across_dense(u2_1, scr[0], dlane)))
     for c in blocks:
         at = cut(c)
@@ -242,7 +244,7 @@
         s2_ref[at, :] = s1p[cut(c, ROWS), :] - 0.25 * wet * change
     leave(1)
     for d, ((ref, sigma, edge, scr), values, more) in enumerate(zip(sides, kept, late)):
-        v1_1, s1_1, s1_2, w0_1, w1_1, r, inverse, h2, v2_2, v2_3, u2_1, u2_2, s2_3 = values
+        v1_1, s1_1, s1_2, w0_1, w1_1, r, inverse, h2, v2_2, v2_3, u2_1, u2_2, s2_3, bump = values
         s2_2, du2_1 = more
         v2_e = row_of(v2p, edge, tiles, ROWS)
         s2_1 = s1_1 - 0.25 * w1_1 * (du2_1 + sigma * (v2_2 - v2_e))
@@ -276,7 +278,7 @@
 
 
 def backward_kernel(
-    gauge_ref, s2_ref, sv_ref, wet_ref, pass_ref, u2_ref, v2_ref, kk_ref, y_ref, yh_ref, u1_ref, v1_ref, t2_ref, t0_ref,
+    gauge_ref, s2_ref, sv_ref, y_ref, pass_ref, u2_ref, v2_ref, kk_ref, wet_ref, yh_ref, u1_ref, v1_ref, t2_ref, t0_ref,
     grad_ref,
     x2p, x2r, pup, pvp, pvr, x1p, x1r, b2s, au1, av1, vs, ms, vt, mt, da, db, dc, dd, *, arrive, leave, shift,
 ):
@@ -344,7 +346,7 @@
         at = cut(c)
         b2 = (1.0 + ms[at, :]) * s2_ref[at, :] - sv_ref[at, :] - vs[at, :]
         b2s[at, :] = b2
-        x2p[cut(c, ROWS), :] = wet_ref[cut(c, total), :].astype(jnp.float32) * b2
+        x2p[cut(c, ROWS), :] = jnp.where(y_ref[at, :] > 0.0, b2, 0.0)
     arrive(5, 6, 7, 8, 9, 10, 11, 12)
     for (sigma, edge, scr), (part, x2_2, y1, w0_1) in zip(sides, kept):
         pvr[pl.ds(edge, tiles, stride=ROWS), :] = (0.25 * sigma) * y1 * (x2_2 - row_of(x2p, edge, tiles, ROWS))
@@ -374,35 +376,36 @@
         grad_ref[cut((c - shift) % tiles), :] = -(energy * t0_ref[at, :] + vs[at, :])
 
 
-def turned_order(count, first):
-    return [(i + first) % count for i in range(count)]
+def turned_order(count, first, stride=1):
+    return [(i * stride + first) % count for i in range(count)]
 
 
 def gauge_table(tile_ref, cell_ref, value_ref, out_ref):
     strips = out_ref.shape[0]
     listed = tile_ref.shape[1]
-    first = STRIP_LEAD * strips // 64
-    hit = (lax.broadcasted_iota(jnp.int32, (strips, listed), 0) + first) % strips == tile_ref[...]
+    strip = (lax.broadcasted_iota(jnp.int32, (strips, listed), 0) * STRIP_STRIDE + STRIP_LEAD) % strips
+    tile = tile_ref[...]
+    hits = [jnp.where(strip + side == tile, 1.0, 0.0) for side in (0, -1, 1)]
     earlier = lax.broadcasted_iota(jnp.int32, (listed, listed), 0) < lax.broadcasted_iota(jnp.int32, (listed, listed), 1)
-    rank = jnp.dot(
-        jnp.where(hit, 1.0, 0.0).astype(jnp.bfloat16), jnp.where(earlier, 1.0, 0.0).astype(jnp.bfloat16),
-        preferred_element_type=jnp.float32,
-    )
-    rank = jnp.where(hit, rank, -1.0)
-    cell = cell_ref[...].astype(jnp.float32) + 1.0
-    value = value_ref[...]
+    ranks = jnp.dot(
+        hits[0].astype(jnp.bfloat16), jnp.where(earlier, 1.0, 0.0).astype(jnp.bfloat16), preferred_element_type=jnp.float32
+    )
+    rank = jnp.sum(hits[0] * ranks, axis=0, keepdims=True).astype(jnp.int32)
+    line = lax.broadcasted_iota(jnp.int32, (LANES, listed), 0)
+    rest = jnp.where(line < 64, cell_ref[...].astype(jnp.float32) + 1.0, value_ref[...])
+    rest = jnp.where((line & 63) == rank, rest, 0.0)
+    hits = jnp.concatenate(hits, axis=0).astype(jnp.bfloat16)
+    table = jnp.zeros((3 * strips, LANES), jnp.float32)
+    for _ in range(3):
+        part = rest.astype(jnp.bfloat16)
+        table = table + lax.dot_general(hits, part, (((1,), (1,)), ((), ())), preferred_element_type=jnp.float32)
+        rest = rest - part.astype(jnp.float32)
     lane = lax.broadcasted_iota(jnp.int32, (strips, LANES), 1)
-    line = (lax.broadcasted_iota(jnp.int32, (strips, LANES), 0) + first) % strips
-    own = jnp.full((strips, LANES), -1.0, jnp.float32)
-    for k in range(8):
-        taken = rank == float(k)
-        cells = jnp.sum(jnp.where(taken, cell, 0.0), axis=1, keepdims=True) - 1.0
-        values = jnp.sum(jnp.where(taken, value, 0.0), axis=1, keepdims=True)
-        own = jnp.where(lane == k, cells, jnp.where(lane == 64 + k, values, own))
-    above = jnp.where(line == 0, -1.0, pltpu.roll(own, 1, 0))
-    below = jnp.where(line == strips - 1, -1.0, pltpu.roll(own, strips - 1, 0))
+    table = [table[i * strips : (i + 1) * strips, :] - jnp.where(lane < 64, 1.0, 0.0) for i in range(3)]
     part = lane & 63
-    out_ref[...] = jnp.where(part < 8, own, jnp.where(part < 16, pltpu.roll(above, 8, 1), pltpu.roll(below, 16, 1)))
+    out_ref[...] = jnp.where(
+        part < 8, table[0], jnp.where(part < 16, pltpu.roll(table[1], 8, 1), pltpu.roll(table[2], 16, 1))
+    )
 
 
 def sum_kernel(x_ref, out_ref):
@@ -416,6 +419,8 @@
 
 def call(body, ins, outs, scratch, name):
     count, given = len(ins), len(outs)
+    taken = [pair[2] if len(pair) > 2 else pair[0].shape[0] for pair in ins]
+    ins = [pair[:2] for pair in ins]
     moved = [i for i, (_, lead) in enumerate(ins) if lead is not HERE]
     copied = [i for i, (shape, kept) in enumerate(outs) if not kept]
 
@@ -425,11 +430,13 @@
         into, out_of = rest[-2:]
         operands, arrivals = list(sources), {}
         for j, i in enumerate(moved):
-            lead, target = ins[i][1], landed[j]
+            lead, target, source = ins[i][1], landed[j], sources[i]
             operands[i] = target
             if lead:
-                target = target.at[pl.ds(lead, sources[i].shape[0])]
-            arrivals[i] = pltpu.make_async_copy(sources[i], target, into.at[j])
+                target = target.at[pl.ds(lead, taken[i])]
+            if taken[i] < source.shape[0]:
+                source = source.at[pl.ds(0, taken[i])]
+            arrivals[i] = pltpu.make_async_copy(source, target, into.at[j])
             arrivals[i].start()
         places, departures = list(results), {}
         for j, i in enumerate(copied):
@@ -438,11 +445,13 @@
 
         def arrive(*which):
             for i in which:
-                arrivals[i].wait()
+                if i in arrivals:
+                    arrivals[i].wait()
 
         def leave(*which):
             for i in which:
-                departures[i].start()
+                if i in departures:
+                    departures[i].start()
 
         body(*operands, *places, *own, arrive=arrive, leave=leave)
         for departure in departures.values():
@@ -454,7 +463,7 @@
         in_specs=[pl.BlockSpec(memory_space=pltpu.VMEM if lead is HERE else pltpu.HBM) for _, lead in ins],
         out_specs=[pl.BlockSpec(memory_space=pltpu.VMEM if kept else pltpu.HBM) for _, kept in outs],
         scratch_shapes=[
-            pltpu.VMEM((ins[i][0].shape[0] + 2 * ins[i][1], ins[i][0].shape[1]), ins[i][0].dtype) for i in moved
+            pltpu.VMEM((taken[i] + 2 * ins[i][1], ins[i][0].shape[1]), ins[i][0].dtype) for i in moved
         ]
         + [pltpu.VMEM(outs[i][0], jnp.float32) for i in copied]
         + [pltpu.VMEM(shape, jnp.float32) for shape in scratch]
@@ -492,25 +501,26 @@
     down, up, send, edges, u1, v1i, q1, k, t0, kr = call(
         prepare_kernel,
         lists + [(s0, ROWS)] + [(x, 0) for x in (depth, rough, u0, v0, wet, survey)],
-        [(packet, True), (packet, True), ((strips, LANES), True), ((2 * len(EDGES) * tiles, LANES), False)]
+        [(packet, True), (packet, True), ((strips, LANES), False), ((2 * EDGES * tiles, LANES), False)]
         + [(field, False)] * 6,
         [padded] * 5 + [field] * 6,
         "prepare",
     )
     from_above = shifted(down, "tile", 1)
     from_below = shifted(up, "tile", -1)
-    gauges = lax.all_to_all(send, "tile", 0, 0, axis_index_groups=[turned_order(strips, STRIP_LEAD * strips // 64)], tiled=True)
+    gauges = lax.all_to_all(send, "tile", 0, 0, axis_index_groups=[turned_order(strips, STRIP_LEAD, STRIP_STRIDE)], tiled=True)
     v1, s2, u2, v2, y, yh, t2, kk, passed = call(
         forward_kernel,
         [(edges, 0), (from_above, HERE), (from_below, HERE)] + [(x, 0) for x in (v1i, q1, wet, u1, k, depth, kr)],
-        [(field, False)] * 8 + [((2 * len(PASS) * tiles, LANES), False)],
+        [(field, True)] * 6 + [(field, False)] * 2 + [((2 * len(PASS) * tiles, LANES), True)],
         [padded] * 4 + [field] * 3 + [dense] * 6,
         "forward",
     )
     order = turned_order(events, EVENT_LEAD * events // 8)
     (grad,) = call(
         functools.partial(backward_kernel, shift=order[0] * (tiles // events)),
-        [(gauges, HERE)] + [(x, 0) for x in (s2, survey, wet, passed, u2, v2, kk, y, yh, u1, v1, t2, t0)],
+        [(gauges, HERE), (s2, HERE), (survey, 0), (y, HERE), (passed, HERE), (u2, HERE), (v2, HERE), (kk, 0)]
+        + [(wet, 0, total), (yh, HERE), (u1, 0), (v1, HERE), (t2, 0), (t0, 0)],
         [(field, True)],
         [padded, field, padded, padded, field, padded, field, field, field, field, field, field]
         + [(6 * tiles, LANES)] * 2 + [dense] * 4,

time: 53.5 us -> 51.8 us (0.968)
  Pallas kernels: 11.1 us -> 9.13 us
    pallas_call x3, Pallas kernels: 10.4 us -> 8.5 us  [call(): pl.pallas_call(kernel, out_shape=[(jax.ShapeDtypeStruct if kept else pltp...]
  transfers between devices with their start and end apart: 3 -> 3, of which waited for: 1 -> 1; matrix products, arithmetic and copies ran while one was open for 0% -> 0% of each run, Pallas kernels for 7% -> 6%
where the time goes in v4:
time: 51.8 us; the launch traced here: 51.5 us
  starting transfers between devices  26.2 us (51%)
  blocking collectives  12.1 us (23%)
  Pallas kernels  9.13 us (18%)
  waiting for transfers between devices  4.01 us (8%)
    all_to_all x1, starting transfers between devices, per_device(): lax.all_to_all(send, 'tile', 0, 0, axis_index_groups=[turned_order(strips...  20.7 us
    all_to_all x1, blocking collectives, per_device(): lax.all_to_all(grad.reshape(events, total // events, LANES), 'event', 0,...  12.1 us
    pallas_call x3, Pallas kernels, call(): pl.pallas_call(kernel, out_shape=[(jax.ShapeDtypeStruct if kept else pltp...  8.5 us
    ppermute x2, starting transfers between devices, shifted(): lax.ppermute(value, axis, [(i, i + steps) for i in range(initial, last)])  5.47 us
    all_to_all x1, waiting for transfers between devices, per_device(): lax.all_to_all(send, 'tile', 0, 0, axis_index_groups=[turned_order(strips...  4.01 us
  transfers between devices with their start and end apart: 3, of which 1 were waited for; matrix products, arithmetic and copies ran while one was open for 0% of the time, Pallas kernels for 6%

profile of v4, /device:TPU:33, one launch (start us, length us, event | category | flops | bytes accessed | tf_op | source)
XLA Modules:
  0.0 51.5 jit_solution(6686337779593951919)
XLA Ops:
  0.0 3.7 %prepare.1 = (f32[1088,128]{1,0:T(8,128)S(1)}, f32[1088,128]{1,0:T(8,128)S(1)}, f32[64,128]{1,0:T(8,128)}, f32[384,128]{1,0:T(8,128)}, f32[512,128]{1,0:T(8,128)...) custom-call(s32[1,256]{1,0:T(1,128)} %bitcast.55, ...), custom_call_target="tpu_custom_call" | custom-call | tf_op jit(solution)/shard_map/prepare/pallas_call | solution.py:460
  3.7 3.5 %collective-permute-start = (f32[1088,128]{1,0:T(8,128)S(1)}, f32[1088,128]{1,0:T(8,128)S(1)}, u32[]{:S(2)}, u32[]{:S(2)}) collective-permute-start(f32[1088,128]{1,0:T(8,128)S(1)} %get-tuple-element.26), channel_id=1, source_target_pairs={{0,1},{1,2},{2,3},{3,4},{4,5},{5,6},{6,7},{7,8},{8,9},{9,10},{10,1... | collective-permute-start | bytes 1671176 | tf_op jit(solution)/shard_map/ppermute | solution.py:486
  7.3 1.9 %collective-permute-start.1 = (f32[1088,128]{1,0:T(8,128)S(1)}, f32[1088,128]{1,0:T(8,128)S(1)}, u32[]{:S(2)}, u32[]{:S(2)}) collective-permute-start(f32[1088,128]{1,0:T(8,128)S(1)} %get-tuple-element.27), channel_id=1, source_target_pairs={{1,0},{2,1},{3,2},{4,3},{5,4},{6,5},{7,6},{8,7},{9,8},{10,9},{11,1... | collective-permute-start | bytes 1671176 | tf_op jit(solution)/shard_map/ppermute | solution.py:486
  9.2 20.7 %all-to-all-start = ((f32[64,1,128]{2,1,0:T(1,128)}), f32[64,1,128]{2,1,0:T(1,128)S(1)}, u32[]{:S(2)}, u32[]{:S(2)}) async-start(f32[64,1,128]{2,1,0:T(1,128)} %bitcast.54), calls=%async_computation | async-start | bytes 65536 | tf_op jit(solution)/shard_map/all_to_all | solution.py:511
  29.9 0.0 collective-permute-done.refs_1_
  29.9 0.0 collective-permute-done.1.refs_2_
  30.0 2.8 %forward.1 = (f32[512,128]{1,0:T(8,128)S(1)}, f32[512,128]{1,0:T(8,128)S(1)}, f32[512,128]{1,0:T(8,128)S(1)}, f32[512,128]{1,0:T(8,128)S(1)}, f32[512,128]{1,0:T...) custom-call(f32[384,128]{1,0:T(8,128)} %get-tuple-element.25.refs_0_, ...), custom_call_target="tpu_custom_call" | custom-call | tf_op jit(solution)/shard_map/forward/pallas_call | solution.py:460
  32.8 4.0 %all-to-all-done = f32[64,1,128]{2,1,0:T(1,128)S(1)} async-done(((f32[64,1,128]{2,1,0:T(1,128)}), f32[64,1,128]{2,1,0:T(1,128)S(1)}, u32[]{:S(2)}, u32[]{:S(2)}) %all-to-all-start) | async-done | bytes 32800 | tf_op jit(solution)/shard_map/all_to_all | solution.py:511
  36.8 2.0 %backward.1 = f32[512,128]{1,0:T(8,128)S(1)} custom-call(f32[64,128]{1,0:T(8,128)S(1)} %bitcast.42, f32[512,128]{1,0:T(8,128)S(1)} %get-tuple-element.33.refs_1_, f32[512,128]{1,0:T(8,128)} %bitcast.47, f32[512,128]{1,0:T(8,128)S(1)} %get-tuple-element.34.refs_3_, f32[1280,128]{1,0:T(8,128)S(1)} %get-tuple-element.35.refs_4_, ...), custom_call_target="tpu_custom_call" | custom-call | tf_op jit(solution)/shard_map/backward/pallas_call | solution.py:460
  38.8 12.1 %all_to_all.16.x_ref = f32[8,64,128]{2,1,0:T(8,128)S(1)} all-to-all(f32[8,64,128]{2,1,0:T(8,128)S(1)} %bitcast.41), channel_id=1, replica_groups={{256,320,384,448,0,64,128,192},{257,321,385,449,1,65,129,193},{258,322,..., dimensions={0} | all-to-all | bytes 524288 | tf_op jit(solution)/shard_map/all_to_all | solution.py:529
  50.9 0.6 %total.1 = f32[8,1024]{1,0:T(8,128)} custom-call(f32[8,64,128]{2,1,0:T(8,128)S(1)} %all_to_all.16.x_ref), custom_call_target="tpu_custom_call" | custom-call | tf_op jit(solution)/shard_map/total/pallas_call | solution.py:530
Async XLA Ops:
  3.7 26.2 %collective-permute-start = (f32[1088,128]{1,0:T(8,128)S(1)}, f32[1088,128]{1,0:T(8,128)S(1)}, u32[]{:S(2)}, u32[]{:S(2)}) collective-permute-start(f32[1088,128]{1,0:T(8,128)S(1)} %get-tuple-element.26), channel_id=1, source_target_pairs={{0,1},{1,2},{2,3},{3,4},{4,5},{5,6},{6,7},{7,8},{8,9},{9,10},{10,1... | collective-permute-start | bytes 1671176 | tf_op jit(solution)/shard_map/ppermute | solution.py:486
  7.3 22.7 %collective-permute-start.1 = (f32[1088,128]{1,0:T(8,128)S(1)}, f32[1088,128]{1,0:T(8,128)S(1)}, u32[]{:S(2)}, u32[]{:S(2)}) collective-permute-start(f32[1088,128]{1,0:T(8,128)S(1)} %get-tuple-element.27), channel_id=1, source_target_pairs={{1,0},{2,1},{3,2},{4,3},{5,4},{6,5},{7,6},{8,7},{9,8},{10,9},{11,1... | collective-permute-start | bytes 1671176 | tf_op jit(solution)/shard_map/ppermute | solution.py:486
  9.2 27.6 %all-to-all-start = ((f32[64,1,128]{2,1,0:T(1,128)}), f32[64,1,128]{2,1,0:T(1,128)S(1)}, u32[]{:S(2)}, u32[]{:S(2)}) async-start(f32[64,1,128]{2,1,0:T(1,128)} %bitcast.54), calls=%async_computation | async-start | bytes 65536 | tf_op jit(solution)/shard_map/all_to_all | solution.py:511

commit v5 on v4

--- a/solution.py
+++ b/solution.py
@@ -78,13 +78,15 @@
     arrive(0, 1, 2)
     gauge_table(tile_ref, cell_ref, value_ref, send_ref)
     leave(2)
-    arrive(3, 4, 5, 6, 7, 8)
     blocks = range(0, tiles, STEP)
 
     def cut(c, lead=0):
         return slice(lead + ROWS * c, lead + ROWS * (c + STEP))
 
-    for c in blocks:
+    arrive(3)
+    for c in blocks:
+        if c * 2 % tiles == 0:
+            arrive(*((2 * c // tiles, i) for i in (4, 5, 6, 7, 8)))
         at = cut(c)
         depth, rough, east, north = h_ref[at, :], rough_ref[at, :], u0_ref[at, :], v0_ref[at, :]
         wet = wet_ref[at, :].astype(jnp.float32)
@@ -118,6 +120,7 @@
         q1_ref[at, :] = q1
         s1p[cut(c, ROWS), :] = q1 - quarter * along(v1p, None, c, STEP, sub)
     leave(6)
+    arrive((2, 8), (3, 8))
     for c in blocks:
         at = cut(c)
         wet = wet_ref[cut(c, total), :].astype(jnp.float32)
@@ -420,6 +423,7 @@
 def call(body, ins, outs, scratch, name):
     count, given = len(ins), len(outs)
     taken = [pair[2] if len(pair) > 2 else pair[0].shape[0] for pair in ins]
+    pieces = [pair[3] if len(pair) > 3 else 1 for pair in ins]
     ins = [pair[:2] for pair in ins]
     moved = [i for i, (_, lead) in enumerate(ins) if lead is not HERE]
     copied = [i for i, (shape, kept) in enumerate(outs) if not kept]
@@ -430,14 +434,18 @@
         into, out_of = rest[-2:]
         operands, arrivals = list(sources), {}
         for j, i in enumerate(moved):
-            lead, target, source = ins[i][1], landed[j], sources[i]
-            operands[i] = target
-            if lead:
-                target = target.at[pl.ds(lead, taken[i])]
-            if taken[i] < source.shape[0]:
-                source = source.at[pl.ds(0, taken[i])]
-            arrivals[i] = pltpu.make_async_copy(source, target, into.at[j])
-            arrivals[i].start()
+            operands[i] = landed[j]
+            size = taken[i] // pieces[i]
+            for part in range(pieces[i]):
+                place = ins[i][1] + part * size
+                target, source = landed[j], sources[i]
+                if size < target.shape[0]:
+                    target = target.at[pl.ds(place, size)]
+                if size < source.shape[0]:
+                    source = source.at[pl.ds(part * size, size)]
+                arrivals[part, i] = pltpu.make_async_copy(source, target, into.at[len(arrivals)])
+        for key in sorted(arrivals):
+            arrivals[key].start()
         places, departures = list(results), {}
         for j, i in enumerate(copied):
             departures[i] = pltpu.make_async_copy(left[j], results[i], out_of.at[j])
@@ -445,7 +453,10 @@
 
         def arrive(*which):
             for i in which:
-                if i in arrivals:
+                for part in range(pieces[i]) if isinstance(i, int) else ():
+                    if (part, i) in arrivals:
+                        arrivals[part, i].wait()
+                if not isinstance(i, int):
                     arrivals[i].wait()
 
         def leave(*which):
@@ -467,7 +478,7 @@
         ]
         + [pltpu.VMEM(outs[i][0], jnp.float32) for i in copied]
         + [pltpu.VMEM(shape, jnp.float32) for shape in scratch]
-        + [pltpu.SemaphoreType.DMA((len(moved),)), pltpu.SemaphoreType.DMA((max(1, len(copied)),))],
+        + [pltpu.SemaphoreType.DMA((sum(pieces[i] for i in moved),)), pltpu.SemaphoreType.DMA((max(1, len(copied)),))],
         name=name,
         compiler_params=pltpu.CompilerParams(vmem_limit_bytes=GRANT),
     )(*(x if lead is HERE else pltpu.with_memory_space_constraint(x, pltpu.HBM) for x, lead in ins))
@@ -500,7 +511,7 @@
     lists = [(x.reshape(listed), 0) for x in (gauge_tiles, gauge_cells, gauge_values)]
     down, up, send, edges, u1, v1i, q1, k, t0, kr = call(
         prepare_kernel,
-        lists + [(s0, ROWS)] + [(x, 0) for x in (depth, rough, u0, v0, wet, survey)],
+        lists + [(s0, ROWS)] + [(x, 0, total, 2) for x in (depth, rough, u0, v0)] + [(wet, 0, 2 * total, 4), (survey, 0)],
         [(packet, True), (packet, True), ((strips, LANES), False), ((2 * EDGES * tiles, LANES), False)]
         + [(field, False)] * 6,
         [padded] * 5 + [field] * 6,

time: 51.8 us -> 51.3 us (level)
  no operation moved by 1% of the time
where the time goes in v5:
time: 51.3 us; the launch traced here: 51 us
  starting transfers between devices  26.2 us (51%)
  blocking collectives  12.1 us (24%)
  Pallas kernels  8.63 us (17%)
  waiting for transfers between devices  4.01 us (8%)
    all_to_all x1, starting transfers between devices, per_device(): lax.all_to_all(send, 'tile', 0, 0, axis_index_groups=[turned_order(strips...  20.7 us
    all_to_all x1, blocking collectives, per_device(): lax.all_to_all(grad.reshape(events, total // events, LANES), 'event', 0,...  12.1 us
    pallas_call x3, Pallas kernels, call(): pl.pallas_call(kernel, out_shape=[(jax.ShapeDtypeStruct if kept else pltp...  8 us
    ppermute x2, starting transfers between devices, shifted(): lax.ppermute(value, axis, [(i, i + steps) for i in range(initial, last)])  5.47 us
    all_to_all x1, waiting for transfers between devices, per_device(): lax.all_to_all(send, 'tile', 0, 0, axis_index_groups=[turned_order(strips...  4.01 us
  transfers between devices with their start and end apart: 3, of which 1 were waited for; matrix products, arithmetic and copies ran while one was open for 0% of the time, Pallas kernels for 6%

profile of v5, /device:TPU:33, one launch (start us, length us, event | category | flops | bytes accessed | tf_op | source)
XLA Modules:
  0.0 51.0 jit_solution(10806218343922095438)
XLA Ops:
  0.0 3.2 %prepare.1 = (f32[1088,128]{1,0:T(8,128)S(1)}, f32[1088,128]{1,0:T(8,128)S(1)}, f32[64,128]{1,0:T(8,128)}, f32[384,128]{1,0:T(8,128)}, f32[512,128]{1,0:T(8,128)...) custom-call(s32[1,256]{1,0:T(1,128)} %bitcast.55, ...), custom_call_target="tpu_custom_call" | custom-call | tf_op jit(solution)/shard_map/prepare/pallas_call | solution.py:471
  3.2 3.5 %collective-permute-start = (f32[1088,128]{1,0:T(8,128)S(1)}, f32[1088,128]{1,0:T(8,128)S(1)}, u32[]{:S(2)}, u32[]{:S(2)}) collective-permute-start(f32[1088,128]{1,0:T(8,128)S(1)} %get-tuple-element.26), channel_id=1, source_target_pairs={{0,1},{1,2},{2,3},{3,4},{4,5},{5,6},{6,7},{7,8},{8,9},{9,10},{10,1... | collective-permute-start | bytes 1671176 | tf_op jit(solution)/shard_map/ppermute | solution.py:497
  6.8 1.9 %collective-permute-start.1 = (f32[1088,128]{1,0:T(8,128)S(1)}, f32[1088,128]{1,0:T(8,128)S(1)}, u32[]{:S(2)}, u32[]{:S(2)}) collective-permute-start(f32[1088,128]{1,0:T(8,128)S(1)} %get-tuple-element.27), channel_id=1, source_target_pairs={{1,0},{2,1},{3,2},{4,3},{5,4},{6,5},{7,6},{8,7},{9,8},{10,9},{11,1... | collective-permute-start | bytes 1671176 | tf_op jit(solution)/shard_map/ppermute | solution.py:497
  8.7 20.7 %all-to-all-start = ((f32[64,1,128]{2,1,0:T(1,128)}), f32[64,1,128]{2,1,0:T(1,128)S(1)}, u32[]{:S(2)}, u32[]{:S(2)}) async-start(f32[64,1,128]{2,1,0:T(1,128)} %bitcast.54), calls=%async_computation | async-start | bytes 65536 | tf_op jit(solution)/shard_map/all_to_all | solution.py:522
  29.4 0.0 collective-permute-done.refs_1_
  29.5 0.0 collective-permute-done.1.refs_2_
  29.5 2.8 %forward.1 = (f32[512,128]{1,0:T(8,128)S(1)}, f32[512,128]{1,0:T(8,128)S(1)}, f32[512,128]{1,0:T(8,128)S(1)}, f32[512,128]{1,0:T(8,128)S(1)}, f32[512,128]{1,0:T...) custom-call(f32[384,128]{1,0:T(8,128)} %get-tuple-element.25.refs_0_, ...), custom_call_target="tpu_custom_call" | custom-call | tf_op jit(solution)/shard_map/forward/pallas_call | solution.py:471
  32.3 4.0 %all-to-all-done = f32[64,1,128]{2,1,0:T(1,128)S(1)} async-done(((f32[64,1,128]{2,1,0:T(1,128)}), f32[64,1,128]{2,1,0:T(1,128)S(1)}, u32[]{:S(2)}, u32[]{:S(2)}) %all-to-all-start) | async-done | bytes 32800 | tf_op jit(solution)/shard_map/all_to_all | solution.py:522
  36.3 2.0 %backward.1 = f32[512,128]{1,0:T(8,128)S(1)} custom-call(f32[64,128]{1,0:T(8,128)S(1)} %bitcast.42, f32[512,128]{1,0:T(8,128)S(1)} %get-tuple-element.33.refs_1_, f32[512,128]{1,0:T(8,128)} %bitcast.47, f32[512,128]{1,0:T(8,128)S(1)} %get-tuple-element.34.refs_3_, f32[1280,128]{1,0:T(8,128)S(1)} %get-tuple-element.35.refs_4_, ...), custom_call_target="tpu_custom_call" | custom-call | tf_op jit(solution)/shard_map/backward/pallas_call | solution.py:471
  38.3 12.1 %all_to_all.16.x_ref = f32[8,64,128]{2,1,0:T(8,128)S(1)} all-to-all(f32[8,64,128]{2,1,0:T(8,128)S(1)} %bitcast.41), channel_id=1, replica_groups={{256,320,384,448,0,64,128,192},{257,321,385,449,1,65,129,193},{258,322,..., dimensions={0} | all-to-all | bytes 524288 | tf_op jit(solution)/shard_map/all_to_all | solution.py:540
  50.4 0.6 %total.1 = f32[8,1024]{1,0:T(8,128)} custom-call(f32[8,64,128]{2,1,0:T(8,128)S(1)} %all_to_all.16.x_ref), custom_call_target="tpu_custom_call" | custom-call | tf_op jit(solution)/shard_map/total/pallas_call | solution.py:541
Async XLA Ops:
  3.2 26.2 %collective-permute-start = (f32[1088,128]{1,0:T(8,128)S(1)}, f32[1088,128]{1,0:T(8,128)S(1)}, u32[]{:S(2)}, u32[]{:S(2)}) collective-permute-start(f32[1088,128]{1,0:T(8,128)S(1)} %get-tuple-element.26), channel_id=1, source_target_pairs={{0,1},{1,2},{2,3},{3,4},{4,5},{5,6},{6,7},{7,8},{8,9},{9,10},{10,1... | collective-permute-start | bytes 1671176 | tf_op jit(solution)/shard_map/ppermute | solution.py:497
  6.8 22.7 %collective-permute-start.1 = (f32[1088,128]{1,0:T(8,128)S(1)}, f32[1088,128]{1,0:T(8,128)S(1)}, u32[]{:S(2)}, u32[]{:S(2)}) collective-permute-start(f32[1088,128]{1,0:T(8,128)S(1)} %get-tuple-element.27), channel_id=1, source_target_pairs={{1,0},{2,1},{3,2},{4,3},{5,4},{6,5},{7,6},{8,7},{9,8},{10,9},{11,1... | collective-permute-start | bytes 1671176 | tf_op jit(solution)/shard_map/ppermute | solution.py:497
  8.7 27.6 %all-to-all-start = ((f32[64,1,128]{2,1,0:T(1,128)}), f32[64,1,128]{2,1,0:T(1,128)S(1)}, u32[]{:S(2)}, u32[]{:S(2)}) async-start(f32[64,1,128]{2,1,0:T(1,128)} %bitcast.54), calls=%async_computation | async-start | bytes 65536 | tf_op jit(solution)/shard_map/all_to_all | solution.py:522

commit v6 on v5

--- a/solution.py
+++ b/solution.py
@@ -68,8 +68,8 @@
 
 def prepare_kernel(
     tile_ref, cell_ref, value_ref, s0p, h_ref, rough_ref, u0_ref, v0_ref, wet_ref, sv_ref,
-    down_ref, up_ref, send_ref, edge_ref, u1_ref, v1_ref, q1_ref, k_ref, t0_ref, kr_ref,
-    u1p, v1p, s1p, u2p, v2p, hh, s2p, b_ref, w0q, w1_ref, rr, *, arrive, leave,
+    down_ref, up_ref, send_ref, edge_ref, u1_ref, v1_ref, t0_ref,
+    k_ref, u1p, v1p, s1p, u2p, v2p, hh, s2p, b_ref, w0q, w1_ref, rr, *, arrive, leave,
 ):
     total = u1_ref.shape[0]
     tiles = total // ROWS
@@ -85,6 +85,8 @@
 
     arrive(3)
     for c in blocks:
+        if c * 2 == tiles:
+            leave((0, 4), (0, 5), (0, 6))
         if c * 2 % tiles == 0:
             arrive(*((2 * c // tiles, i) for i in (4, 5, 6, 7, 8)))
         at = cut(c)
@@ -105,21 +107,18 @@
         v1_ref[at, :] = v1
         b_ref[at, :] = b
         k_ref[at, :] = k
-        kr_ref[at, :] = kr
         t0_ref[at, :] = kr * speed * inverse
         w0q[at, :] = 0.25 * wet
     for i, (ref, lead) in enumerate(((s0p, ROWS), (v1_ref, 0), (b_ref, 0))):
         for j, row in enumerate((0, ROWS - 1)):
             first = (j * EDGES + i) * tiles
             edge_ref[first : first + tiles, :] = row_of(ref, row, tiles, lead)
-    leave(3, 4, 5, 7, 8, 9)
+    leave((1, 4), (1, 5), (1, 6), 3)
     for c in blocks:
         at = cut(c)
         quarter = w0q[at, :]
         q1 = s0p[cut(c, ROWS), :] - quarter * across(u1p, c, STEP, lane)
-        q1_ref[at, :] = q1
         s1p[cut(c, ROWS), :] = q1 - quarter * along(v1p, None, c, STEP, sub)
-    leave(6)
     arrive((2, 8), (3, 8))
     for c in blocks:
         at = cut(c)
@@ -153,15 +152,15 @@
 
 
 def forward_kernel(
-    edge_ref, top_ref, bot_ref, v1i_ref, q1_ref, wet_ref, u1_ref, k_ref, h_ref, kr_ref,
+    edge_ref, top_ref, bot_ref, v1i_ref, s0_ref, wet_ref, u1p, h_ref, rough_ref,
     v1_ref, s2_ref, u2_ref, v2_ref, y_ref, yh_ref, t2_ref, kk_ref, pass_ref,
     v1p, s1p, u2p, v2p, v1r, s1r, v2r, da, db, dc, dd, de, df, *, arrive, leave,
 ):
-    total = u1_ref.shape[0]
+    total = v1i_ref.shape[0]
     tiles = total // ROWS
     lane, sub = masks(ROWS * STEP)
     dlane = lax.broadcasted_iota(jnp.int32, (tiles, LANES), 1)
-    clear_ends(v1p, s1p, u2p, v2p, da, db, dc, dd, de, df)
+    clear_ends(u1p, v1p, s1p, u2p, v2p, da, db, dc, dd, de, df)
     blocks = range(0, tiles, STEP)
 
     def cut(c, lead=0):
@@ -202,14 +201,15 @@
         s2_3 = got(ref, 3, "s2") + (0.25 * sigma) * jnp.where(h3 > 0.0, 1.0, 0.0) * (v2_2 - v2i_2)
         u2_1 = (w1_1 * u1_1 - r * across_dense(s1_1, scr[1], dlane)) * inverse
         kept.append((v1_1, s1_1, s1_2, w0_1, w1_1, r, inverse, h2, v2_2, v2_3, u2_1, u2_2, s2_3, bump))
-    arrive(4, 5)
+    arrive(4, 5, 6)
     for c in blocks:
         at = cut(c)
         quarter = 0.25 * wet_ref[at, :].astype(jnp.float32)
         v1_ref[at, :] = v1p[cut(c, ROWS), :]
-        s1p[cut(c, ROWS), :] = q1_ref[at, :] - quarter * along(v1p, v1r, c, STEP, sub)
+        change = across(u1p, c, STEP, lane) + along(v1p, v1r, c, STEP, sub)
+        s1p[cut(c, ROWS), :] = s0_ref[at, :] - quarter * change
     leave(0)
-    arrive(6, 7, 8, 9)
+    arrive(7, 8)
     late = []
     for (ref, sigma, edge, scr), values in zip(sides, kept):
         v1_1, s1_1, s1_2, w0_1, w1_1, r, inverse, h2, v2_2, v2_3, u2_1, u2_2, s2_3, bump = values
@@ -221,14 +221,16 @@
         late.append((s2_2, across_dense(u2_1, scr[0], dlane)))
     for c in blocks:
         at = cut(c)
-        east, north = u1_ref[at, :], v1_ref[at, :]
+        east, north = u1p[cut(c, ROWS), :], v1_ref[at, :]
         speed2 = east * east + north * north + 1.0
         slow = lax.rsqrt(speed2)
         speed = speed2 * slow
-        k = k_ref[at, :]
+        depth, rough = h_ref[at, :], rough_ref[at, :]
+        kr = 4.0 * rough * jnp.exp((-4.0 / 3.0) * jnp.log(depth))
+        k = 0.5 * kr * rough
         inverse = 1.0 / (1.0 + k * speed)
         y = wet_ref[cut(c, total), :].astype(jnp.float32) * inverse
-        yh = 0.2 * h_ref[at, :] * y
+        yh = 0.2 * depth * y
         u2 = y * east - yh * across(s1p, c, STEP, lane)
         v2 = y * north - yh * along(s1p, s1r, c, STEP, sub)
         u2p[cut(c, ROWS), :] = u2
@@ -237,7 +239,7 @@
         v2_ref[at, :] = v2
         y_ref[at, :] = y
         yh_ref[at, :] = yh
-        t2_ref[at, :] = kr_ref[at, :] * speed * inverse
+        t2_ref[at, :] = kr * speed * inverse
         kk_ref[at, :] = k * inverse * slow
     leave(2, 3, 4, 5, 6, 7)
     for c in blocks:
@@ -425,6 +427,8 @@
     taken = [pair[2] if len(pair) > 2 else pair[0].shape[0] for pair in ins]
     pieces = [pair[3] if len(pair) > 3 else 1 for pair in ins]
     ins = [pair[:2] for pair in ins]
+    shares = [pair[2] if len(pair) > 2 else 1 for pair in outs]
+    outs = [pair[:2] for pair in outs]
     moved = [i for i, (_, lead) in enumerate(ins) if lead is not HERE]
     copied = [i for i, (shape, kept) in enumerate(outs) if not kept]
 
@@ -448,7 +452,12 @@
             arrivals[key].start()
         places, departures = list(results), {}
         for j, i in enumerate(copied):
-            departures[i] = pltpu.make_async_copy(left[j], results[i], out_of.at[j])
+            size = outs[i][0][0] // shares[i]
+            for part in range(shares[i]):
+                target, source = results[i], left[j]
+                if shares[i] > 1:
+                    target, source = target.at[pl.ds(part * size, size)], source.at[pl.ds(part * size, size)]
+                departures[part, i] = pltpu.make_async_copy(source, target, out_of.at[len(departures)])
             places[i] = left[j]
 
         def arrive(*which):
@@ -461,8 +470,9 @@
 
         def leave(*which):
             for i in which:
-                if i in departures:
-                    departures[i].start()
+                for key in [(0, i)] if isinstance(i, int) else [i]:
+                    if key in departures:
+                        departures[key].start()
 
         body(*operands, *places, *own, arrive=arrive, leave=leave)
         for departure in departures.values():
@@ -478,7 +488,7 @@
         ]
         + [pltpu.VMEM(outs[i][0], jnp.float32) for i in copied]
         + [pltpu.VMEM(shape, jnp.float32) for shape in scratch]
-        + [pltpu.SemaphoreType.DMA((sum(pieces[i] for i in moved),)), pltpu.SemaphoreType.DMA((max(1, len(copied)),))],
+        + [pltpu.SemaphoreType.DMA((sum(pieces[i] for i in moved),)), pltpu.SemaphoreType.DMA((max(1, sum(shares[i] for i in copied)),))],
         name=name,
         compiler_params=pltpu.CompilerParams(vmem_limit_bytes=GRANT),
     )(*(x if lead is HERE else pltpu.with_memory_space_constraint(x, pltpu.HBM) for x, lead in ins))
@@ -509,12 +519,12 @@
     packet = (len(SENT) * tiles, LANES)
     listed = (1, gauge_cells.shape[1])
     lists = [(x.reshape(listed), 0) for x in (gauge_tiles, gauge_cells, gauge_values)]
-    down, up, send, edges, u1, v1i, q1, k, t0, kr = call(
+    down, up, send, edges, u1, v1i, t0 = call(
         prepare_kernel,
         lists + [(s0, ROWS)] + [(x, 0, total, 2) for x in (depth, rough, u0, v0)] + [(wet, 0, 2 * total, 4), (survey, 0)],
         [(packet, True), (packet, True), ((strips, LANES), False), ((2 * EDGES * tiles, LANES), False)]
-        + [(field, False)] * 6,
-        [padded] * 5 + [field] * 6,
+        + [(field, False, 2)] * 3,
+        [field] + [padded] * 5 + [field] * 6,
         "prepare",
     )
     from_above = shifted(down, "tile", 1)
@@ -522,7 +532,7 @@
     gauges = lax.all_to_all(send, "tile", 0, 0, axis_index_groups=[turned_order(strips, STRIP_LEAD, STRIP_STRIDE)], tiled=True)
     v1, s2, u2, v2, y, yh, t2, kk, passed = call(
         forward_kernel,
-        [(edges, 0), (from_above, HERE), (from_below, HERE)] + [(x, 0) for x in (v1i, q1, wet, u1, k, depth, kr)],
+        [(edges, 0), (from_above, HERE), (from_below, HERE)] + [(x, 0) for x in (v1i, s0, wet)] + [(u1, ROWS), (depth, 0), (rough, 0)],
         [(field, True)] * 6 + [(field, False)] * 2 + [((2 * len(PASS) * tiles, LANES), True)],
         [padded] * 4 + [field] * 3 + [dense] * 6,
         "forward",

time: 51.3 us -> 50.9 us (level)
  no operation moved by 1% of the time
where the time goes in v6:
time: 50.9 us; the launch traced here: 50.6 us
  starting transfers between devices  26.2 us (51%)
  blocking collectives  12.1 us (24%)
  Pallas kernels  8.26 us (16%)
  waiting for transfers between devices  3.95 us (8%)
    all_to_all x1, starting transfers between devices, per_device(): lax.all_to_all(send, 'tile', 0, 0, axis_index_groups=[turned_order(strips...  20.7 us
    all_to_all x1, blocking collectives, per_device(): lax.all_to_all(grad.reshape(events, total // events, LANES), 'event', 0,...  12.1 us
    pallas_call x3, Pallas kernels, call(): pl.pallas_call(kernel, out_shape=[(jax.ShapeDtypeStruct if kept else pltp...  7.63 us
    ppermute x2, starting transfers between devices, shifted(): lax.ppermute(value, axis, [(i, i + steps) for i in range(initial, last)])  5.47 us
    all_to_all x1, waiting for transfers between devices, per_device(): lax.all_to_all(send, 'tile', 0, 0, axis_index_groups=[turned_order(strips...  3.95 us
  transfers between devices with their start and end apart: 3, of which 1 were waited for; matrix products, arithmetic and copies ran while one was open for 0% of the time, Pallas kernels for 6%

profile of v6, /device:TPU:33, one launch (start us, length us, event | category | flops | bytes accessed | tf_op | source)
XLA Modules:
  0.0 50.6 jit_solution(12137983308856825269)
XLA Ops:
  0.0 2.8 %prepare.1 = (f32[1088,128]{1,0:T(8,128)S(1)}, f32[1088,128]{1,0:T(8,128)S(1)}, f32[64,128]{1,0:T(8,128)}, f32[384,128]{1,0:T(8,128)}, f32[512,128]{1,0:T(8,128)...) custom-call(s32[1,256]{1,0:T(1,128)} %bitcast.57, s32[1,256]{1,0:T(1,128)} %refs_1_.1, f32[1,256]{1,0:T(1,128)} %refs_2_.1, ...), custom_call_target="tpu_custom_call" | custom-call | tf_op jit(solution)/shard_map/prepare/pallas_call | solution.py:481
  2.8 3.5 %collective-permute-start = (f32[1088,128]{1,0:T(8,128)S(1)}, f32[1088,128]{1,0:T(8,128)S(1)}, u32[]{:S(2)}, u32[]{:S(2)}) collective-permute-start(f32[1088,128]{1,0:T(8,128)S(1)} %get-tuple-element.23), channel_id=1, source_target_pairs={{0,1},{1,2},{2,3},{3,4},{4,5},{5,6},{6,7},{7,8},{8,9},{9,10},{10,1... | collective-permute-start | bytes 1671176 | tf_op jit(solution)/shard_map/ppermute | solution.py:507
  6.3 1.9 %collective-permute-start.1 = (f32[1088,128]{1,0:T(8,128)S(1)}, f32[1088,128]{1,0:T(8,128)S(1)}, u32[]{:S(2)}, u32[]{:S(2)}) collective-permute-start(f32[1088,128]{1,0:T(8,128)S(1)} %get-tuple-element.24), channel_id=1, source_target_pairs={{1,0},{2,1},{3,2},{4,3},{5,4},{6,5},{7,6},{8,7},{9,8},{10,9},{11,1... | collective-permute-start | bytes 1671176 | tf_op jit(solution)/shard_map/ppermute | solution.py:507
  8.3 20.7 %all-to-all-start = ((f32[64,1,128]{2,1,0:T(1,128)}), f32[64,1,128]{2,1,0:T(1,128)S(1)}, u32[]{:S(2)}, u32[]{:S(2)}) async-start(f32[64,1,128]{2,1,0:T(1,128)} %bitcast.56), calls=%async_computation | async-start | bytes 65536 | tf_op jit(solution)/shard_map/all_to_all | solution.py:532
  29.0 0.0 collective-permute-done.refs_1_
  29.0 0.0 collective-permute-done.1.refs_2_
  29.0 2.9 %forward.1 = (f32[512,128]{1,0:T(8,128)S(1)}, f32[512,128]{1,0:T(8,128)S(1)}, f32[512,128]{1,0:T(8,128)S(1)}, f32[512,128]{1,0:T(8,128)S(1)}, f32[512,128]{1,0:T...) custom-call(f32[384,128]{1,0:T(8,128)} %get-tuple-element.22.refs_0_, ...), custom_call_target="tpu_custom_call" | custom-call | tf_op jit(solution)/shard_map/forward/pallas_call | solution.py:481
  31.9 3.9 %all-to-all-done = f32[64,1,128]{2,1,0:T(1,128)S(1)} async-done(((f32[64,1,128]{2,1,0:T(1,128)}), f32[64,1,128]{2,1,0:T(1,128)S(1)}, u32[]{:S(2)}, u32[]{:S(2)}) %all-to-all-start) | async-done | bytes 32800 | tf_op jit(solution)/shard_map/all_to_all | solution.py:532
  35.9 2.0 %backward.1 = f32[512,128]{1,0:T(8,128)S(1)} custom-call(f32[64,128]{1,0:T(8,128)S(1)} %bitcast.42, f32[512,128]{1,0:T(8,128)S(1)} %get-tuple-element.27.refs_1_, f32[512,128]{1,0:T(8,128)} %bitcast.53, f32[512,128]{1,0:T(8,128)S(1)} %get-tuple-element.28.refs_3_, f32[1280,128]{1,0:T(8,128)S(1)} %get-tuple-element.29.refs_4_, ...), custom_call_target="tpu_custom_call" | custom-call | tf_op jit(solution)/shard_map/backward/pallas_call | solution.py:481
  37.9 12.1 %all_to_all.16.x_ref = f32[8,64,128]{2,1,0:T(8,128)S(1)} all-to-all(f32[8,64,128]{2,1,0:T(8,128)S(1)} %bitcast.41), channel_id=1, replica_groups={{256,320,384,448,0,64,128,192},{257,321,385,449,1,65,129,193},{258,322,..., dimensions={0} | all-to-all | bytes 524288 | tf_op jit(solution)/shard_map/all_to_all | solution.py:550
  49.9 0.6 %total.1 = f32[8,1024]{1,0:T(8,128)} custom-call(f32[8,64,128]{2,1,0:T(8,128)S(1)} %all_to_all.16.x_ref), custom_call_target="tpu_custom_call" | custom-call | tf_op jit(solution)/shard_map/total/pallas_call | solution.py:551
Async XLA Ops:
  2.8 26.2 %collective-permute-start = (f32[1088,128]{1,0:T(8,128)S(1)}, f32[1088,128]{1,0:T(8,128)S(1)}, u32[]{:S(2)}, u32[]{:S(2)}) collective-permute-start(f32[1088,128]{1,0:T(8,128)S(1)} %get-tuple-element.23), channel_id=1, source_target_pairs={{0,1},{1,2},{2,3},{3,4},{4,5},{5,6},{6,7},{7,8},{8,9},{9,10},{10,1... | collective-permute-start | bytes 1671176 | tf_op jit(solution)/shard_map/ppermute | solution.py:507
  6.3 22.7 %collective-permute-start.1 = (f32[1088,128]{1,0:T(8,128)S(1)}, f32[1088,128]{1,0:T(8,128)S(1)}, u32[]{:S(2)}, u32[]{:S(2)}) collective-permute-start(f32[1088,128]{1,0:T(8,128)S(1)} %get-tuple-element.24), channel_id=1, source_target_pairs={{1,0},{2,1},{3,2},{4,3},{5,4},{6,5},{7,6},{8,7},{9,8},{10,9},{11,1... | collective-permute-start | bytes 1671176 | tf_op jit(solution)/shard_map/ppermute | solution.py:507
  8.3 27.6 %all-to-all-start = ((f32[64,1,128]{2,1,0:T(1,128)}), f32[64,1,128]{2,1,0:T(1,128)S(1)}, u32[]{:S(2)}, u32[]{:S(2)}) async-start(f32[64,1,128]{2,1,0:T(1,128)} %bitcast.56), calls=%async_computation | async-start | bytes 65536 | tf_op jit(solution)/shard_map/all_to_all | solution.py:532

commit v7 on v6

--- a/solution.py
+++ b/solution.py
@@ -11,7 +11,7 @@
 STEP = 4
 GRANT = 16 * 1024 * 1024
 HERE = None
-STRIP_LEAD = 42
+STRIP_LEAD = 44
 STRIP_STRIDE = 1
 EVENT_LEAD = 4
 RIM1 = ("s0", "v1", "b", "s1", "r", "u1", "k", "sv")

time: 50.9 us -> 50.9 us (level)
  waiting for transfers between devices: 3.95 us -> 5.35 us
  starting transfers between devices: 26.2 us -> 24.8 us
    all_to_all x1, starting transfers between devices: 20.7 us -> 19.4 us  [per_device(): lax.all_to_all(send, 'tile', 0, 0, axis_index_groups=[turned_order(strips...]
    all_to_all x1, waiting for transfers between devices: 3.95 us -> 5.34 us  [per_device(): lax.all_to_all(send, 'tile', 0, 0, axis_index_groups=[turned_order(strips...]
where the time goes in v7:
time: 50.9 us; the launch traced here: 50.6 us
  starting transfers between devices  24.8 us (49%)
  blocking collectives  12.1 us (24%)
  Pallas kernels  8.26 us (16%)
  waiting for transfers between devices  5.35 us (11%)
    all_to_all x1, starting transfers between devices, per_device(): lax.all_to_all(send, 'tile', 0, 0, axis_index_groups=[turned_order(strips...  19.4 us
    all_to_all x1, blocking collectives, per_device(): lax.all_to_all(grad.reshape(events, total // events, LANES), 'event', 0,...  12.1 us
    pallas_call x3, Pallas kernels, call(): pl.pallas_call(kernel, out_shape=[(jax.ShapeDtypeStruct if kept else pltp...  7.63 us
    ppermute x2, starting transfers between devices, shifted(): lax.ppermute(value, axis, [(i, i + steps) for i in range(initial, last)])  5.47 us
    all_to_all x1, waiting for transfers between devices, per_device(): lax.all_to_all(send, 'tile', 0, 0, axis_index_groups=[turned_order(strips...  5.34 us
  transfers between devices with their start and end apart: 3, of which 1 were waited for; matrix products, arithmetic and copies ran while one was open for 0% of the time, Pallas kernels for 6%

profile of v7, /device:TPU:33, one launch (start us, length us, event | category | flops | bytes accessed | tf_op | source)
XLA Modules:
  0.0 50.6 jit_solution(16875933942543041844)
XLA Ops:
  0.0 2.8 %prepare.1 = (f32[1088,128]{1,0:T(8,128)S(1)}, f32[1088,128]{1,0:T(8,128)S(1)}, f32[64,128]{1,0:T(8,128)}, f32[384,128]{1,0:T(8,128)}, f32[512,128]{1,0:T(8,128)...) custom-call(s32[1,256]{1,0:T(1,128)} %bitcast.57, s32[1,256]{1,0:T(1,128)} %refs_1_.1, f32[1,256]{1,0:T(1,128)} %refs_2_.1, ...), custom_call_target="tpu_custom_call" | custom-call | tf_op jit(solution)/shard_map/prepare/pallas_call | solution.py:481
  2.8 3.5 %collective-permute-start = (f32[1088,128]{1,0:T(8,128)S(1)}, f32[1088,128]{1,0:T(8,128)S(1)}, u32[]{:S(2)}, u32[]{:S(2)}) collective-permute-start(f32[1088,128]{1,0:T(8,128)S(1)} %get-tuple-element.23), channel_id=1, source_target_pairs={{0,1},{1,2},{2,3},{3,4},{4,5},{5,6},{6,7},{7,8},{8,9},{9,10},{10,1... | collective-permute-start | bytes 1671176 | tf_op jit(solution)/shard_map/ppermute | solution.py:507
  6.3 1.9 %collective-permute-start.1 = (f32[1088,128]{1,0:T(8,128)S(1)}, f32[1088,128]{1,0:T(8,128)S(1)}, u32[]{:S(2)}, u32[]{:S(2)}) collective-permute-start(f32[1088,128]{1,0:T(8,128)S(1)} %get-tuple-element.24), channel_id=1, source_target_pairs={{1,0},{2,1},{3,2},{4,3},{5,4},{6,5},{7,6},{8,7},{9,8},{10,9},{11,1... | collective-permute-start | bytes 1671176 | tf_op jit(solution)/shard_map/ppermute | solution.py:507
  8.3 19.4 %all-to-all-start = ((f32[64,1,128]{2,1,0:T(1,128)}), f32[64,1,128]{2,1,0:T(1,128)S(1)}, u32[]{:S(2)}, u32[]{:S(2)}) async-start(f32[64,1,128]{2,1,0:T(1,128)} %bitcast.56), calls=%async_computation | async-start | bytes 65536 | tf_op jit(solution)/shard_map/all_to_all | solution.py:532
  27.6 0.0 collective-permute-done.refs_1_
  27.6 0.0 collective-permute-done.1.refs_2_
  27.6 2.9 %forward.1 = (f32[512,128]{1,0:T(8,128)S(1)}, f32[512,128]{1,0:T(8,128)S(1)}, f32[512,128]{1,0:T(8,128)S(1)}, f32[512,128]{1,0:T(8,128)S(1)}, f32[512,128]{1,0:T...) custom-call(f32[384,128]{1,0:T(8,128)} %get-tuple-element.22.refs_0_, ...), custom_call_target="tpu_custom_call" | custom-call | tf_op jit(solution)/shard_map/forward/pallas_call | solution.py:481
  30.5 5.3 %all-to-all-done = f32[64,1,128]{2,1,0:T(1,128)S(1)} async-done(((f32[64,1,128]{2,1,0:T(1,128)}), f32[64,1,128]{2,1,0:T(1,128)S(1)}, u32[]{:S(2)}, u32[]{:S(2)}) %all-to-all-start) | async-done | bytes 32800 | tf_op jit(solution)/shard_map/all_to_all | solution.py:532
  35.9 2.0 %backward.1 = f32[512,128]{1,0:T(8,128)S(1)} custom-call(f32[64,128]{1,0:T(8,128)S(1)} %bitcast.42, f32[512,128]{1,0:T(8,128)S(1)} %get-tuple-element.27.refs_1_, f32[512,128]{1,0:T(8,128)} %bitcast.53, f32[512,128]{1,0:T(8,128)S(1)} %get-tuple-element.28.refs_3_, f32[1280,128]{1,0:T(8,128)S(1)} %get-tuple-element.29.refs_4_, ...), custom_call_target="tpu_custom_call" | custom-call | tf_op jit(solution)/shard_map/backward/pallas_call | solution.py:481
  37.9 12.1 %all_to_all.16.x_ref = f32[8,64,128]{2,1,0:T(8,128)S(1)} all-to-all(f32[8,64,128]{2,1,0:T(8,128)S(1)} %bitcast.41), channel_id=1, replica_groups={{256,320,384,448,0,64,128,192},{257,321,385,449,1,65,129,193},{258,322,..., dimensions={0} | all-to-all | bytes 524288 | tf_op jit(solution)/shard_map/all_to_all | solution.py:550
  49.9 0.6 %total.1 = f32[8,1024]{1,0:T(8,128)} custom-call(f32[8,64,128]{2,1,0:T(8,128)S(1)} %all_to_all.16.x_ref), custom_call_target="tpu_custom_call" | custom-call | tf_op jit(solution)/shard_map/total/pallas_call | solution.py:551
Async XLA Ops:
  2.8 24.8 %collective-permute-start = (f32[1088,128]{1,0:T(8,128)S(1)}, f32[1088,128]{1,0:T(8,128)S(1)}, u32[]{:S(2)}, u32[]{:S(2)}) collective-permute-start(f32[1088,128]{1,0:T(8,128)S(1)} %get-tuple-element.23), channel_id=1, source_target_pairs={{0,1},{1,2},{2,3},{3,4},{4,5},{5,6},{6,7},{7,8},{8,9},{9,10},{10,1... | collective-permute-start | bytes 1671176 | tf_op jit(solution)/shard_map/ppermute | solution.py:507
  6.3 21.3 %collective-permute-start.1 = (f32[1088,128]{1,0:T(8,128)S(1)}, f32[1088,128]{1,0:T(8,128)S(1)}, u32[]{:S(2)}, u32[]{:S(2)}) collective-permute-start(f32[1088,128]{1,0:T(8,128)S(1)} %get-tuple-element.24), channel_id=1, source_target_pairs={{1,0},{2,1},{3,2},{4,3},{5,4},{6,5},{7,6},{8,7},{9,8},{10,9},{11,1... | collective-permute-start | bytes 1671176 | tf_op jit(solution)/shard_map/ppermute | solution.py:507
  8.3 27.6 %all-to-all-start = ((f32[64,1,128]{2,1,0:T(1,128)}), f32[64,1,128]{2,1,0:T(1,128)S(1)}, u32[]{:S(2)}, u32[]{:S(2)}) async-start(f32[64,1,128]{2,1,0:T(1,128)} %bitcast.56), calls=%async_computation | async-start | bytes 65536 | tf_op jit(solution)/shard_map/all_to_all | solution.py:532
